TPU v7x, 512 devices: a whole 4x8x8 slice. The times are simulated.
512 devices in a mesh: head: 4 (over x), tensor: 16 (over y, z_hi), dp: 8 (over z_lo, core).
Axes of the slice: x: 4, y: 8, z: 8 (z_hi: 2, z_lo: 4; z = z_hi * 4 + z_lo), core: 2. Of those that a mesh axis runs over, the one named last changes fastest.
Arguments:
- trunk_hidden: bfloat16 [384, 5120], P('dp', 'tensor'), may hold values from -60 to 60
- next_embeds: bfloat16 [4, 384, 5120], P('head', 'dp', 'tensor'), may hold values from -6 to 6
- combine_weight: bfloat16 [4, 10240, 5120], P('head', 'dp', 'tensor'), may hold values from -0.0625 to 0.0625
- final_gain: float32 [5120], P('tensor'), may hold values from 0.5 to 1.5
- unembed_weight: bfloat16 [16384, 5120], P('dp', 'tensor'), may hold values from -32 to 32
- target_ids: int32 [4, 384], P('head'), may hold values from 0 to 16383
- loss_scale: float32 [4, 384], P('head'), may hold values from 2 to 32
Outputs:
- trunk_grad: float32 [384, 5120], P('dp', 'tensor')
- embed_grad: float32 [4, 384, 5120], P('head', 'dp', 'tensor')
- combine_grad: float32 [4, 10240, 5120], P('head', 'dp', 'tensor')
- unembed_grad: float32 [8, 4, 512, 5120], P('dp', 'head', None, 'tensor')
All inputs are finite; a program needn't handle non-finite values.
Results may differ from a plain program's by a relative error of at most 0.02.
Values may be sent and summed in bfloat16 or wider, within the bound.
A program may use at most 64 MiB of HBM per device.

v0:
```python
import jax
import jax.numpy as jnp
from jax import lax
from jax.sharding import PartitionSpec as P

D = 5120


epsilon = 1e-05


def contract_rows(left, right):
    return lax.dot_general(
        left, right, (((0,), (0,)), ((), ())), preferred_element_type=jnp.float32
    )


def contract_cols(left, right):
    return lax.dot_general(
        left, right, (((1,), (1,)), ((), ())), preferred_element_type=jnp.float32
    )


def local(
    trunk_hidden, next_embeds, combine_weight, final_gain, unembed_weight, target_ids, loss_scale
):
    rows, part_width = trunk_hidden.shape
    vocab_part = unembed_weight.shape[0]
    weight_block = combine_weight[0]
    trunk_whole, embed_whole = (
        lax.all_gather(trunk_hidden, "tensor", axis=1, tiled=True),
        lax.all_gather(next_embeds[0], "tensor", axis=1, tiled=True),
    )
    trunk_float = trunk_whole.astype(jnp.float32)
    embed_float = embed_whole.astype(jnp.float32)
    trunk_scale = lax.rsqrt(jnp.sum(trunk_float * trunk_float, axis=1) / D + epsilon)
    embed_scale = lax.rsqrt(jnp.sum(embed_float * embed_float, axis=1) / D + epsilon)
    trunk_normed = trunk_float * trunk_scale[:, None]
    embed_normed = embed_float * embed_scale[:, None]
    joined = jnp.concatenate(
        [trunk_normed.astype(jnp.bfloat16), embed_normed.astype(jnp.bfloat16)], axis=1
    )
    feature_start = lax.axis_index("tensor") * part_width
    trunk_local = lax.dynamic_slice_in_dim(trunk_normed, feature_start, part_width, 1)
    embed_local = lax.dynamic_slice_in_dim(embed_normed, feature_start, part_width, 1)
    blocks = lax.all_to_all(joined, "dp", split_axis=1, concat_axis=0, tiled=True)
    weight_whole = lax.all_gather(weight_block, "dp", axis=0, tiled=True)
    projected = jnp.dot(joined, weight_whole, preferred_element_type=jnp.float32)
    mixed = trunk_hidden.astype(jnp.float32) + projected
    mixed_sums = lax.psum(jnp.sum(mixed * mixed, axis=1), "tensor")
    mixed_scale = lax.rsqrt(mixed_sums / D + epsilon)
    mixed_normed = mixed * mixed_scale[:, None]
    normed_out = (mixed_normed * final_gain[None, :]).astype(jnp.bfloat16)
    normed_all = lax.all_gather(normed_out, "dp", axis=0, tiled=True)
    partial_logits = contract_cols(normed_all, unembed_weight)
    logits = lax.psum(partial_logits, "tensor")
    row_targets = target_ids[0]
    row_weights = loss_scale[0]
    largest = lax.pmax(jnp.max(logits, axis=1), "dp")
    shifted = jnp.exp(logits - largest[:, None])
    summed = lax.psum(jnp.sum(shifted, axis=1), "dp")
    probs = shifted / summed[:, None]
    vocab_ids = (
        lax.broadcasted_iota(jnp.int32, (1, vocab_part), 1) + lax.axis_index("dp") * vocab_part
    )
    hits = (vocab_ids == row_targets[:, None]).astype(jnp.float32)
    grad_local = (row_weights[:, None] * (probs - hits)).astype(jnp.bfloat16)
    grad_normed = lax.psum_scatter(
        jnp.dot(grad_local, unembed_weight, preferred_element_type=jnp.float32).astype(
            jnp.bfloat16
        ),
        "dp",
        scatter_dimension=0,
        tiled=True,
    ).astype(jnp.float32)
    vocab_term = contract_rows(grad_local, normed_all).astype(jnp.bfloat16)
    vocab_total = lax.psum_scatter(vocab_term, "head", scatter_dimension=0, tiled=True).astype(
        jnp.float32
    )
    unembed_grad = vocab_total.reshape(1, 1, vocab_total.shape[0], part_width)
    scaled_grad = grad_normed * final_gain[None, :]
    grad_dots = lax.psum(jnp.sum(scaled_grad * mixed_normed, axis=1), "tensor")
    grad_mixed = mixed_scale[:, None] * (scaled_grad - mixed_normed * (grad_dots / D)[:, None])
    grad_mixed_low = grad_mixed.astype(jnp.bfloat16)
    grad_all = lax.all_gather(grad_mixed_low, "dp", axis=0, tiled=True)
    combine_grad = contract_rows(blocks, grad_all)[None]
    joined_part = contract_cols(grad_mixed_low, weight_whole)
    joined_grad = lax.psum_scatter(
        joined_part.reshape(rows, 2, D).astype(jnp.bfloat16),
        "tensor",
        scatter_dimension=2,
        tiled=True,
    ).astype(jnp.float32)
    trunk_side = joined_grad[:, 0]
    embed_side = joined_grad[:, 1]
    trunk_dots, embed_dots = lax.psum(
        (jnp.sum(trunk_side * trunk_local, axis=1), jnp.sum(embed_side * embed_local, axis=1)),
        "tensor",
    )
    trunk_term = trunk_scale[:, None] * (trunk_side - trunk_local * (trunk_dots / D)[:, None])
    embed_grad = (embed_scale[:, None] * (embed_side - embed_local * (embed_dots / D)[:, None]))[
        None
    ]
    trunk_grad = lax.psum((grad_mixed + trunk_term).astype(jnp.bfloat16), "head").astype(
        jnp.float32
    )
    return (trunk_grad, embed_grad, combine_grad, unembed_grad)


def solution(mesh):
    in_specs = (
        P("dp", "tensor"),
        P("head", "dp", "tensor"),
        P("head", "dp", "tensor"),
        P("tensor"),
        P("dp", "tensor"),
        P("head", None),
        P("head", None),
    )
    out_specs = (
        P("dp", "tensor"),
        P("head", "dp", "tensor"),
        P("head", "dp", "tensor"),
        P("dp", "head", None, "tensor"),
    )
    return jax.shard_map(local, mesh=mesh, in_specs=in_specs, out_specs=out_specs, check_vma=False)
```

profile of v0, /device:TPU:56, one launch (start us, length us, event | category | flops | bytes accessed | tf_op | source)
XLA Modules:
  0.0 1118.6 jit_solution(15558136090920150623)
XLA Ops:
  7.2 0.7 all-gather.5.cloned.1.call-update
  8.0 73.1 %all-gather.2 = bf16[16,320,48]{1,2,0:T(8,128)(2,1)S(1)} all-gather(bf16[1,320,48]{1,2,0:T(8,128)(2,1)} %bitcast.77), channel_id=1, replica_groups=mesh['head'=4,'tensor'=16,'dp'=8] {'tensor'}, dimensions={0}, use_global_device_ids=true | all-gather | bytes 522240 | tf_op jit(solution)/shard_map/all_gather | solution.py:31
  81.0 0.1 copy.15
  81.1 0.3 reshape.52
  81.5 0.2 copy.16
  81.7 156.5 %all-gather = bf16[1,48,5120]{1,0,2:T(2,128)(2,1)} all-gather(bf16[1,48,320]{1,0,2:T(2,128)(2,1)S(1)} %copy.16), channel_id=2, replica_groups=mesh['head'=4,'tensor'=16,'dp'=8] {'tensor'}, dimensions={2}, use_global_device_ids=true | all-gather | bytes 522240 | tf_op jit(solution)/shard_map/all_gather | solution.py:32
  238.2 4.7 copy.17
  243.0 0.2 fusion.7
  243.2 0.2 multiply_reduce_fusion
  243.4 1.2 convert_multiply_fusion
  244.6 1.2 convert_bitcast_fusion
  245.8 5.1 multiply_reduce_fusion.3
  250.9 50.6 %psum.49 = f32[48]{0:T(128)S(1)} all-reduce(f32[48]{0:T(128)S(1)} %get-tuple-element.14), channel_id=1, replica_groups=mesh['head'=4,'tensor'=16,'dp'=8] {'tensor'}, use_global_device_ids=true, to_apply=%region_3.0 | all-reduce | flops 48 | bytes 384 | tf_op jit(solution)/shard_map/psum | solution.py:50
  301.5 0.1 multiply_convert_fusion.1
  301.6 18.9 %all_gather.18 = bf16[384,320]{1,0:T(8,128)(2,1)S(1)} all-gather(bf16[48,320]{1,0:T(8,128)(2,1)S(1)} %multiply_convert_fusion.1), channel_id=1, replica_groups=mesh['head'=4,'tensor'=16,'dp'=8] {'dp'}, dimensions={0}, use_global_device_ids=true | all-gather | bytes 276480 | tf_op jit(solution)/shard_map/all_gather | solution.py:54
  320.5 0.7 copy-done.2
  321.2 2.6 fusion.15
  323.9 0.6 copy-done.7
  324.6 336.9 %all-reduce.3.cloned.1.call-done = f32[384,2048]{1,0:T(8,128)} async-done(((f32[384,2048]{1,0:T(8,128)}), f32[384,2048]{1,0:T(8,128)}) %all-reduce.3.cloned.1.call-update) | async-done | bytes 3145744 | tf_op jit(solution)/shard_map/psum | solution.py:56
  661.5 2.1 reduce_max.9
  663.6 13.6 %pmax.7 = f32[384]{0:T(512)S(1)} all-reduce(f32[384]{0:T(512)S(1)} %reduce_max.9), channel_id=1, replica_groups=mesh['head'=4,'tensor'=16,'dp'=8] {'dp'}, use_global_device_ids=true, to_apply=%region_6.0 | all-reduce | flops 384 | bytes 3072 | tf_op jit(solution)/shard_map/pmax | solution.py:59
  677.2 2.5 fusion.3
  679.7 13.6 %psum.51 = f32[384]{0:T(512)S(1)} all-reduce(f32[384]{0:T(512)S(1)} %fusion.3), channel_id=1, replica_groups=mesh['head'=4,'tensor'=16,'dp'=8] {'dp'}, use_global_device_ids=true, to_apply=%region_8.0 | all-reduce | flops 384 | bytes 3072 | tf_op jit(solution)/shard_map/psum | solution.py:61
  693.3 2.9 multiply_convert_fusion
  696.1 1.7 convolution_convert_fusion.2
  697.9 44.3 %reduce-scatter.6.cloned.1.call-done = bf16[48,320]{1,0:T(8,128)(2,1)} async-done(((bf16[384,320]{1,0:T(8,128)(2,1)}), bf16[48,320]{1,0:T(8,128)(2,1)}) %reduce-scatter.6.cloned.1.call-update) | async-done | bytes 30736 | tf_op jit(solution)/shard_map/reduce_scatter | solution.py:68
  742.2 0.9 multiply_reduce_fusion.2
  743.2 48.7 %psum.52 = f32[48]{0:T(128)S(1)} all-reduce(f32[48]{0:T(128)S(1)} %multiply_reduce_fusion.2), channel_id=1, replica_groups=mesh['head'=4,'tensor'=16,'dp'=8] {'tensor'}, use_global_device_ids=true, to_apply=%region_11.0 | all-reduce | flops 48 | bytes 384 | tf_op jit(solution)/shard_map/psum | solution.py:82
  791.8 0.9 fusion.13
  792.7 5.1 convolution_convert_fusion
  797.8 3.7 convert_element_type.64
  801.5 7.5 copy.20
  808.9 5.4 reshape.53
  814.4 2.9 convolution_convert_fusion.1
  817.3 1.1 pad_maximum_fusion
  818.4 1.0 copy.25
  819.4 3.6 all-to-all-start
  823.0 34.0 %all_gather.19 = bf16[384,320]{1,0:T(8,128)(2,1)S(1)} all-gather(bf16[48,320]{1,0:T(8,128)(2,1)S(1)} %fusion.13), channel_id=1, replica_groups=mesh['head'=4,'tensor'=16,'dp'=8] {'dp'}, dimensions={0}, use_global_device_ids=true | all-gather | bytes 276480 | tf_op jit(solution)/shard_map/all_gather | solution.py:85
  857.0 1.8 convolution_bitcast_fusion
  858.8 183.7 %reduce-scatter.10.cloned.1.call-done = bf16[320,96]{1,0:T(8,128)(2,1)} async-done(((bf16[5120,96]{1,0:T(8,128)(2,1)}), bf16[320,96]{1,0:T(8,128)(2,1)}) %reduce-scatter.10.cloned.1.call-update) | async-done | bytes 61456
  1042.5 1.0 reshape.54
  1043.5 0.1 copy.21
  1043.7 1.2 multiply_reduce_fusion.1
  1044.9 45.7 %all-reduce = (f32[48]{0:T(128)S(1)}, f32[48]{0:T(128)S(1)}) all-reduce(f32[48]{0:T(128)S(1)} %get-tuple-element.5, f32[48]{0:T(128)S(1)} %get-tuple-element.4), channel_id=1, replica_groups=mesh['head'=4,'tensor'=16,'dp'=8] {'tensor'}, use_global_device_ids=true, to_apply=%region_14.0 | all-reduce | flops 96 | bytes 768 | tf_op jit(solution)/shard_map/psum | solution.py:96
  1090.6 1.7 multiply_bitcast_fusion
  1092.3 17.2 %psum.54 = bf16[48,320]{1,0:T(8,128)(2,1)S(1)} all-reduce(bf16[48,320]{1,0:T(8,128)(2,1)S(1)} %get-tuple-element.13), channel_id=1, replica_groups=mesh['head'=4,'tensor'=16,'dp'=8] {'head'}, use_global_device_ids=true, to_apply=%region_15.0 | all-reduce | flops 15360 | bytes 61440 | tf_op jit(solution)/shard_map/psum | solution.py:104
  1109.6 0.6 convert_element_type.67
  1110.2 1.9 bitcast_convert_fusion
  (37 shorter events, 0.4 us)
Async XLA Ops:
  7.2 314.0 %copy-start = (bf16[2048,320]{0,1:T(8,128)(2,1)S(1)}, bf16[2048,320]{0,1:T(8,128)(2,1)}, u32[]{:S(2)}) copy-start(bf16[2048,320]{0,1:T(8,128)(2,1)} %param.11) | copy-start | bytes 3932164
  7.2 74.3 %copy-start.5 = (bf16[1,48,320]{2,1,0:T(8,128)(2,1)S(1)}, bf16[1,48,320]{2,1,0:T(8,128)(2,1)}, u32[]{:S(2)}) copy-start(bf16[1,48,320]{2,1,0:T(8,128)(2,1)} %param.8) | copy-start | bytes 92164
  7.2 238.6 %all-gather.5.cloned.1.call-start = ((), (), s32[]{:S(2)}) async-start(), calls=%async_computation.7 | async-start | bytes 7372800 | tf_op jit(solution)/shard_map/all_gather | solution.py:47
  7.9 653.6 %all-reduce.3.cloned.1.call-start = ((), (), s32[]{:S(2)}) async-start(), calls=%async_computation.4 | async-start | bytes 6291456 | tf_op jit(solution)/shard_map/psum | solution.py:56
  243.2 2.6 copy-start.4
  245.8 5.1 copy-start.1
  245.8 55.7 %copy-start.6 = (f32[320]{0:T(512)S(1)}, f32[320]{0:T(512)}, u32[]{:S(2)}) copy-start(f32[320]{0:T(512)} %param.10) | copy-start | bytes 3844
  320.5 0.7 copy-start.2
  323.8 0.7 copy-start.7
  323.8 0.7 copy-start.8
  323.9 418.3 %reduce-scatter.6.cloned.1.call-start = ((), (), s32[]{:S(2)}) async-start(), calls=%async_computation.5 | async-start | bytes 331776 | tf_op jit(solution)/shard_map/reduce_scatter | solution.py:68
  697.9 344.7 %reduce-scatter.10.cloned.1.call-start = ((), (), s32[]{:S(2)}) async-start(), calls=%async_computation.8 | async-start | bytes 1392640
  814.3 295.9 %reduce-scatter.8.cloned.1.call-start = ((), (), s32[]{:S(2)}) async-start(), calls=%async_computation.6 | async-start | bytes 1638400 | tf_op jit(solution)/shard_map/reduce_scatter | solution.py:77
  819.4 37.6 %all-to-all-start = ((bf16[48,8,1280]{2,0,1:T(8,128)(2,1)}), bf16[48,8,1280]{2,0,1:T(8,128)(2,1)S(1)}, u32[]{:S(2)}, u32[]{:S(2)}) async-start(bf16[48,8,1280]{2,0,1:T(8,128)(2,1)} %bitcast.72), calls=%async_computation.1 | async-start | bytes 1966080 | tf_op jit(solution)/shard_map/all_to_all | solution.py:46
  823.0 267.6 %copy-start.3 = (bf16[48,320]{1,0:T(8,128)(2,1)S(1)}, bf16[48,320]{1,0:T(8,128)(2,1)}, u32[]{:S(2)}) copy-start(bf16[48,320]{1,0:T(8,128)(2,1)} %reduce-scatter.6.cloned.1.call-done) | copy-start | bytes 92164
Sparse Core Ops, SparseCore 0:
  10.1 159.1 all-gather.4
  324.0 337.4 all-reduce.2
  698.0 44.1 reduce-scatter.5
  814.5 228.0 reduce-scatter.9
  1045.2 25.9 reduce-scatter.7
where the time goes:
time: 1120 us
  waiting for transfers between devices  566 us (51%)
  blocking collectives  472 us (42%)
  local copies, waits for them, and re-layouts  25.4 us (2%)
  matrix products  19.3 us (2%)
  other arithmetic  18.7 us (2%)
  between operations  14 us (1%)
    psum x1, waiting for transfers between devices, local(): logits = lax.psum(partial_logits, 'tensor')  337 us
    unnamed x6, waiting for transfers between devices  184 us
    all_gather x1, blocking collectives, local(): lax.all_gather(next_embeds[0], 'tensor', axis=1, tiled=True)  157 us
    all_gather x1, blocking collectives, local(): lax.all_gather(trunk_hidden, 'tensor', axis=1, tiled=True)  73.1 us
    psum x1, blocking collectives, local(): mixed_sums = lax.psum(jnp.sum(mixed * mixed, axis=1), 'tensor')  50.6 us
    psum x1, blocking collectives, local(): grad_dots = lax.psum(jnp.sum(scaled_grad * mixed_normed, axis=1), 'tensor')  48.7 us
    psum x1, blocking collectives, local(): lax.psum((jnp.sum(trunk_side * trunk_local, axis=1), jnp.sum(embed_side *...  45.7 us
    reduce_scatter x1, waiting for transfers between devices, local(): lax.psum_scatter(jnp.dot(grad_local, unembed_weight, preferred_element_ty...  44.3 us
  transfers between devices with their start and end apart: 6, of which 3 were waited for; matrix products, arithmetic and copies ran while one was open for 2% of the time, Pallas kernels for 0%

commit v1 on v0

v1 whole, which is shorter than its diff:
```python
import jax
import jax.numpy as jnp
from jax import lax
from jax.experimental import pallas as pl
from jax.experimental.pallas import tpu as pltpu
from jax.sharding import PartitionSpec as P

D = 5120
EPS = 1e-05
R = 48
N = 192
C = 320
CP = 384
V = 2048
VC = 256
MESH = pl.DeviceIdType.MESH
HI = lax.Precision.HIGHEST
f32 = jnp.float32
bf16 = jnp.bfloat16


def dot(left, right, a, b, precision=None):
    return lax.dot_general(
        left, right, (((a,), (b,)), ((), ())), precision=precision, preferred_element_type=f32
    )


def kernel(
    xb, w, u, gain, tgt, wt,
    tg, eg, cg, ug,
    W2, XB, XS, PB, R2, T, Y8, MX, UP, LP, RL, MSC, YN, YS,
    SB0, SY0, SB1, SY1, SB2, SZ2, GA, GS, GN, NB, NR, SG, DCB, DCR, SB3, SY3,
    GMF, GML, GMS, JP, RJ, SD, PRE, XPR, SB4, SY4, SB5, S7, VB, VR, VSB, VSR,
    ssem, rsem, lsem,
):
    h = lax.axis_index("head")
    t = lax.axis_index("tensor")
    d = lax.axis_index("dp")
    y, zh = lax.div(t, 2), lax.rem(t, 2)
    zl, c = lax.div(d, 2), lax.rem(d, 2)
    z = zh * 4 + zl
    oc, ozh = 1 - c, 1 - zh

    def dev(h_=None, y_=None, z_=None, c_=None):
        h_ = h if h_ is None else h_
        y_ = y if y_ is None else y_
        z_ = z if z_ is None else z_
        c_ = c if c_ is None else c_
        return (h_, y_ * 2 + lax.div(z_, 4), lax.rem(z_, 4) * 2 + c_)

    def add(value, step, size):
        return lax.rem(value + (step + size), size)

    sib = dev(c_=oc)
    right, left = dev(y_=add(y, 1, 8)), dev(y_=add(y, -1, 8))
    me = dev()

    counts = {"s": 0, "r": 0}

    def slots(n):
        first = counts["s"]
        counts["s"] += n
        return first

    finals = []

    def copy(src, dst, s, r, to):
        return pltpu.make_async_remote_copy(
            src_ref=src, dst_ref=dst, send_sem=ssem.at[s], recv_sem=rsem.at[r],
            device_id=to, device_id_type=MESH,
        )

    def when(cond, body):
        if cond is None:
            body()
        else:
            pl.when(cond)(body)

    def send(src, dst, s, r, to, cond=None):
        when(cond, lambda: copy(src(), dst(), s, r, to).start())
        finals.append((cond, lambda: copy(src(), dst(), s, r, to).wait_send()))

    def recv(dst, r):
        copy(dst, dst, 0, r, me).wait_recv()

    lane = lax.broadcasted_iota(jnp.int32, (R, CP), 1)
    e8 = (
        lax.broadcasted_iota(jnp.int32, (8, 128), 0) == lax.broadcasted_iota(jnp.int32, (8, 128), 1)
    ).astype(f32)

    def pick(x, at):
        ids = lax.broadcasted_iota(jnp.int32, x.shape, x.ndim - 1)
        return jnp.sum(jnp.where(ids == at, x, 0.0), axis=-1, keepdims=True)

    def to_rows(first, second=None):
        ids = lax.broadcasted_iota(jnp.int32, (first.shape[0], 128), 1)
        v = jnp.where(ids == 0, first, 0.0)
        if second is not None:
            v = jnp.where(ids == 1, second, v)
        return dot(e8, v, 1, 1, HI)

    def to_cols(rows):
        return dot(rows, e8, 0, 0, HI)

    def widen(value, extra):
        T[:, 0:C] = value
        return jnp.where(lane >= C, extra, T[...])

    barrier = pltpu.get_barrier_semaphore()
    peers = [dev(y_=add(y, j, 8)) for j in range(1, 8)]
    peers += [dev(z_=add(z, j, 8)) for j in range(1, 8)]
    peers += [dev(h_=add(h, j, 4)) for j in range(1, 4)]
    peers += [dev(h_=add(h, j, 4), z_=ozh * 4 + zl) for j in range(1, 4)]
    peers += [sib, dev(z_=ozh * 4 + zl, c_=oc)]
    for to in peers:
        pl.semaphore_signal(barrier, inc=1, device_id=to, device_id_type=MESH)
    own_w = pltpu.make_async_copy(w, W2.at[c], lsem.at[0])
    own_w.start()
    T[...] = jnp.zeros_like(T)
    for ref in (SB0, SB1, SB2, SB3, SB4, SB5):
        ref[...] = jnp.zeros_like(ref)
    PB[...] = jnp.zeros_like(PB)
    pl.semaphore_wait(barrier, len(peers))

    yq, ym = lax.div(y, 4), lax.rem(y, 4)
    hf = lax.rem(zl, 2)
    in_half = hf == yq
    a_s, a_r = slots(4), slots(8)
    for kind in range(2):
        for zh_to in range(2):
            z_to = zh_to * 4 + kind * 2 + yq
            send(
                lambda kind=kind: xb.at[kind], lambda: XB.at[ym, z],
                a_s + kind * 2 + zh_to, a_r + z, dev(z_=z_to), z_to != z,
            )

            def keep(kind=kind):
                XB[ym, z] = xb[kind]

            pl.when(z_to == z)(keep)
    w_s = slots(1)
    send(lambda: w, lambda: W2.at[c], w_s, w_s, sib)

    owner = c == zh
    donor = c != zh
    u_q, u_f, u_x, u_d, u_b = slots(4), slots(1), slots(4), slots(1), slots(4)
    own_u = lambda: pltpu.make_async_copy(u, UP.at[zh], lsem.at[1])
    pl.when(owner)(lambda: own_u().start())

    @pl.when(in_half)
    def _():
        for j in range(1, 8):
            zs = add(z, j, 8)
            recv(XB.at[ym, zs], a_r + zs)

    mine = pl.ds(h * 512, 512)
    send(lambda: u.at[mine], lambda: UP.at[zh, mine], u_d, u_q + h, dev(z_=ozh * 4 + zl), donor)

    b_s = slots(16)
    for i in range(8):
        for way in range(2):
            s = add(y, -i, 8) if way == 0 else add(y, i, 8)
            k = lax.rem(s, 4)
            cond = lax.div(s, 4) == hf
            for unit in range(2):
                part = pl.ds(way * 4 + unit * 2, 2)
                idx = b_s + (way * 4 + k) * 2 + unit
                if i > 0:
                    pl.when(cond)(lambda: recv(XB.at[k, part], idx))
                if i < 7:
                    send(
                        lambda k=k, part=part: XB.at[k, part], lambda k=k, part=part: XB.at[k, part],
                        idx, idx, right if way == 0 else left, cond,
                    )

    send(lambda: u, lambda: UP.at[zh], u_f, u_f, sib, owner)
    pl.when(owner)(lambda: recv(UP.at[ozh, mine], u_q + h))
    for j in range(1, 4):
        send(
            lambda: UP.at[ozh, mine], lambda: UP.at[ozh, mine], u_x + j, u_q + h,
            dev(h_=add(h, j, 4)), owner,
        )
    send(lambda: UP.at[ozh, mine], lambda: UP.at[ozh, mine], u_b, u_q + h, sib, owner)

    own_w.wait()
    recv(W2.at[oc], w_s)
    acc = jnp.zeros((N, C), f32)
    squares = jnp.zeros((N, 1), f32)
    for q in range(8):
        block = XB[q // 2, (q % 2) * 4 : (q % 2) * 4 + 4].reshape(N, C)
        acc = acc + dot(block, W2[q // 4, (q % 4) * C : (q % 4 + 1) * C, :], 1, 0)
        wide = block.astype(f32)
        squares = squares + jnp.sum(wide * wide, axis=1, keepdims=True)
    PB[:, :, 0:C] = acc.reshape(4, R, C)
    lane3 = lax.broadcasted_iota(jnp.int32, (4, R, CP), 2)
    PB[...] = jnp.where(lane3 >= C, squares.reshape(4, R, 1), PB[...])
    p_s, p_r = slots(4), slots(4)
    for j in range(1, 4):
        zt = add(zl, j, 4)
        send(
            lambda zt=zt: PB.at[zt], lambda: R2.at[zl], p_s + j, p_r + zl, dev(z_=zh * 4 + zt)
        )
    R2[zl] = PB[zl]
    x_s = slots(1)
    send(lambda: XB.at[pl.ds(2 * oc, 2)], lambda: XS, x_s, x_s, sib)
    for j in range(1, 4):
        zt = add(zl, j, 4)
        recv(R2.at[zt], p_r + zt)
    from_trunk = R2[0] + R2[1]
    from_embed = R2[2] + R2[3]
    trunk = xb[0].astype(f32)
    embed = xb[1].astype(f32)
    trunk_scale = lax.rsqrt(pick(from_trunk, C) / D + EPS)
    embed_scale = lax.rsqrt(pick(from_embed, C) / D + EPS)
    mixed = trunk + trunk_scale * from_trunk[:, 0:C] + embed_scale * from_embed[:, 0:C]
    MX[zl] = mixed
    gains = gain[...]
    total = jnp.sum(mixed * mixed, axis=1, keepdims=True)
    high = total.astype(bf16).astype(f32)
    middle = (total - high).astype(bf16).astype(f32)
    low = total - high - middle
    pieces = jnp.where(lane == C, high, jnp.where(lane == C + 1, middle, low))
    Y8[z] = widen(mixed * gains, pieces).astype(bf16)
    y_s, y_r = slots(8), slots(8)
    for j in range(1, 8):
        send(lambda: Y8.at[z], lambda: Y8.at[z], y_s + j, y_r + z, dev(z_=add(z, j, 8)))
    m_s, m_r = slots(4), slots(4)
    for j in range(1, 4):
        send(
            lambda: MX.at[zl], lambda: MX.at[zl], m_s + j, m_r + zl, dev(z_=zh * 4 + add(zl, j, 4))
        )
    for j in range(1, 4):
        ht = add(h, j, 4)
        quarter = pl.ds(ht * 512, 512)
        pl.when(owner)(lambda: recv(UP.at[ozh, quarter], u_q + ht))
        send(
            lambda quarter=quarter: UP.at[ozh, quarter], lambda quarter=quarter: UP.at[ozh, quarter],
            u_b + j, u_q + ht, sib, owner,
        )
    for j in range(1, 8):
        zs = add(z, j, 8)
        recv(Y8.at[zs], y_r + zs)

    wide = Y8[...].astype(f32)
    ids = lax.broadcasted_iota(jnp.int32, wide.shape, 2)
    split = jnp.sum(
        jnp.where((ids >= C) & (ids < C + 3), wide, 0.0), axis=2, keepdims=True
    )
    part_squares = (split[0:4] + split[4:8]).reshape(N, 1)
    SB0[:, 0:N] = to_rows(part_squares)
    s0_s, s0_r = slots(8), slots(8)
    for j in range(1, 8):
        send(lambda: SB0, lambda: SY0.at[y], s0_s + j, s0_r + y, dev(y_=add(y, j, 8)))
    SY0[y] = SB0[...]

    @pl.when(owner)
    def _():
        own_u().wait()

    @pl.when(donor)
    def _():
        recv(UP.at[zh], u_f)
        for j in range(4):
            recv(UP.at[ozh, pl.ds(j * 512, 512)], u_q + j)

    y0 = Y8[0:4].reshape(N, CP)[:, 0:C]
    y1 = Y8[4:8].reshape(N, CP)[:, 0:C]

    def logits_block(at, carry):
        rows = pl.ds(pl.multiple_of(at * VC, VC), VC)
        LP[at] = dot(y0, UP[0, rows, :], 1, 1) + dot(y1, UP[1, rows, :], 1, 1)
        return carry

    lax.fori_loop(0, 8, logits_block, 0)
    l_s = slots(32)
    for i in range(8):
        for way in range(2):
            to = add(y, -1 - i, 8) if way == 0 else add(y, 1 + i, 8)
            for unit in range(2):
                rows = slice(way * 96 + unit * 48, way * 96 + unit * 48 + 48)
                idx = l_s + (way * 8 + i) * 2 + unit
                if i > 0:
                    recv(RL.at[to, rows], idx - 2)
                    LP[to, rows] = LP[to, rows] + RL[to, rows]
                if i < 7:
                    send(
                        lambda to=to, rows=rows: LP.at[to, rows],
                        lambda to=to, rows=rows: RL.at[to, rows],
                        idx, idx, right if way == 0 else left,
                    )
    for j in range(1, 8):
        ys = add(y, j, 8)
        recv(SY0.at[ys], s0_r + ys)
    all_squares = to_cols(jnp.sum(SY0[...], axis=0)[:, 0:N])
    mixed_scale = lax.rsqrt(pick(all_squares, 0) / D + EPS)
    MSC[...] = jnp.broadcast_to(mixed_scale, (N, 128)).reshape(4, R, 128)
    YN[0] = (y0.astype(f32) * mixed_scale).astype(bf16)
    YN[1] = (y1.astype(f32) * mixed_scale).astype(bf16)
    n_s = slots(1)
    send(lambda: YN.at[oc], lambda: YS, n_s, n_s, sib)

    logits = LP[y] * mixed_scale
    largest = jnp.max(logits, axis=1, keepdims=True)
    summed = jnp.sum(jnp.exp(logits - largest), axis=1, keepdims=True)
    SB1[:, 0:N] = to_rows(largest, summed)
    s1_s, s1_r = slots(8), slots(8)
    for j in range(1, 8):
        send(lambda: SB1, lambda: SY1.at[y], s1_s + j, s1_r + y, dev(y_=add(y, j, 8)))
    SY1[y] = SB1[...]

    def merge(ref):
        every = ref[...]
        top = jnp.max(every[:, 0:1, :], axis=0)
        whole = jnp.sum(every[:, 1:2, :] * jnp.exp(every[:, 0:1, :] - top[None]), axis=0)
        ids = lax.broadcasted_iota(jnp.int32, (8, VC), 0)
        return jnp.where(ids == 0, top, jnp.where(ids == 1, whole, 0.0))

    for j in range(1, 8):
        ys = add(y, j, 8)
        recv(SY1.at[ys], s1_r + ys)
    SB2[...] = merge(SY1)
    s2_s, s2_r = slots(8), slots(8)
    for j in range(1, 8):
        send(lambda: SB2, lambda: SZ2.at[z], s2_s + j, s2_r + z, dev(z_=add(z, j, 8)))
    SZ2[z] = SB2[...]
    for j in range(1, 8):
        zs = add(z, j, 8)
        recv(SZ2.at[zs], s2_r + zs)
    stats = to_cols(merge(SZ2)[:, 0:N])
    probs = jnp.exp(logits - pick(stats, 0)) / pick(stats, 1)
    vocab_ids = (zl * 4096 + zh * 2048 + y * VC) + lax.broadcasted_iota(jnp.int32, (N, VC), 1)
    hits = (vocab_ids == tgt[...]).astype(f32)
    GA[y] = (wt[...] * (probs - hits)).astype(bf16)

    g_s = slots(20)
    for i in range(5):
        for way in range(2):
            s = add(y, -i, 8) if way == 0 else add(y, i, 8)
            for half in range(2):
                rows = slice(half * 96, half * 96 + 96)
                idx = g_s + (way * 5 + i) * 2 + half
                if i > 0 and (i < 4 or half == way):
                    recv(GA.at[s, rows], idx - 2)
                if i < 3 or (i == 3 and half == way):
                    send(
                        lambda s=s, rows=rows: GA.at[s, rows], lambda s=s, rows=rows: GA.at[s, rows],
                        idx, idx, right if way == 0 else left,
                    )
    gs_s = slots(1)
    send(lambda: GA, lambda: GS, gs_s, gs_s, sib)

    GN[...] = jnp.zeros_like(GN)

    def normed_block(at, carry):
        rows = pl.ds(pl.multiple_of(at * VC, VC), VC)
        grads = GA[at]
        for zc in range(2):
            GN[zc] += dot(grads, UP[zc, rows, :], 1, 0)
        return carry

    lax.fori_loop(0, 8, normed_block, 0)
    NB[...] = GN[...].astype(bf16).reshape(8, R, C)
    n8_s, n8_r = slots(8), slots(8)
    for j in range(1, 8):
        zt = add(z, j, 8)
        send(lambda zt=zt: NB.at[zt], lambda: NR.at[z], n8_s + j, n8_r + z, dev(z_=zt))
    NR[z] = NB[z]

    recv(GS, gs_s)
    recv(YS, n_s)
    normed_mine = YN[c]
    normed_sib = YS[...]

    def vocab_block(at, carry):
        value = dot(GA[at], normed_mine, 0, 0) + dot(GS[at], normed_sib, 0, 0)
        VB[lax.div(at, 2), pl.ds(pl.multiple_of(lax.rem(at, 2) * VC, VC), VC), :] = value.astype(bf16)
        return carry

    lax.fori_loop(0, 8, vocab_block, 0)
    v_s, v_r = slots(4), slots(4)
    for j in range(1, 4):
        ht = add(h, j, 4)
        send(lambda ht=ht: VB.at[ht], lambda: VR.at[h], v_s + j, v_r + h, dev(h_=ht))
    VR[h] = VB[h]

    for j in range(1, 8):
        zs = add(z, j, 8)
        recv(NR.at[zs], n8_r + zs)
    for j in range(1, 4):
        zs = add(zl, j, 4)
        recv(MX.at[zs], m_r + zs)
    grad_normed = jnp.sum(NR[...].astype(f32), axis=0)
    scaled = grad_normed * gains
    inner = jnp.sum(scaled * (MX[zl] * MSC[zl][:, 0:1]), axis=1, keepdims=True)
    SG[zl] = widen(
        scaled, jnp.where(lane == C, inner, jnp.where(lane == C + 1, trunk_scale, embed_scale))
    )
    DCB[...] = jnp.broadcast_to(inner, (R, 128))
    d_s, d_r, e_s, e_r = slots(4), slots(4), slots(4), slots(4)
    for j in range(1, 4):
        zt = add(zl, j, 4)
        send(lambda: SG.at[zl], lambda: SG.at[zl], d_s + j, d_r + zl, dev(z_=zh * 4 + zt))
    for j in range(4):
        zt = add(zl, j, 4)
        send(lambda: DCB, lambda: DCR.at[zl], e_s + j, e_r + zl, dev(z_=ozh * 4 + zt))
    for j in range(1, 4):
        zs = add(zl, j, 4)
        recv(SG.at[zs], d_r + zs)
    for j in range(4):
        zs = add(zl, j, 4)
        recv(DCR.at[zs], e_r + zs)
    inner_part = (pick(SG[...], C) + pick(DCR[...], 0)).reshape(N, 1)
    SB3[:, 0:N] = to_rows(inner_part)
    s3_s, s3_r = slots(8), slots(8)
    for j in range(1, 8):
        send(lambda: SB3, lambda: SY3.at[y], s3_s + j, s3_r + y, dev(y_=add(y, j, 8)))
    SY3[y] = SB3[...]
    for j in range(1, 8):
        ys = add(y, j, 8)
        recv(SY3.at[ys], s3_r + ys)
    inner_all = pick(to_cols(jnp.sum(SY3[...], axis=0)[:, 0:N]), 0)
    mixed_normed = MX[...].reshape(N, C) * MSC[...].reshape(N, 128)[:, 0:1]
    scales = MSC[...].reshape(N, 128)[:, 0:1]
    grad_mixed = scales * (
        SG[...].reshape(N, CP)[:, 0:C] - mixed_normed * (inner_all / D)
    )
    GMF[...] = grad_mixed.reshape(4, R, C)
    grad_low = grad_mixed.astype(bf16)
    gathered = SG[...].reshape(N, CP)
    joined_scale = jnp.where(lax.div(zl, 2) == 0, pick(gathered, C + 1), pick(gathered, C + 2))
    grad_joined = (grad_mixed * joined_scale).astype(bf16)
    GML[...] = grad_joined
    c_s = slots(1)
    send(lambda: GML, lambda: GMS, c_s, c_s, sib)

    for q in range(8):
        value = dot(grad_low, W2[q // 4, (q % 4) * C : (q % 4 + 1) * C, :], 1, 1)
        JP[q // 2, (q % 2) * 4 : (q % 2) * 4 + 4] = value.astype(bf16).reshape(4, R, C)
    j_s = slots(16)
    for i in range(8):
        for way in range(2):
            to = add(y, -1 - i, 8) if way == 0 else add(y, 1 + i, 8)
            k = lax.rem(to, 4)
            cond = lax.div(to, 4) == hf
            for unit in range(2):
                part = pl.ds(way * 4 + unit * 2, 2)
                idx = j_s + (way * 4 + k) * 2 + unit

                def take():
                    recv(RJ.at[k, part], idx)
                    JP[k, part] = (JP[k, part].astype(f32) + RJ[k, part].astype(f32)).astype(bf16)

                if i > 0:
                    pl.when(cond)(take)
                if i < 7:
                    send(
                        lambda k=k, part=part: JP.at[k, part], lambda k=k, part=part: RJ.at[k, part],
                        idx, idx, right if way == 0 else left, cond,
                    )
    kind_mine = lax.div(zl, 2)
    k_s, k_r = slots(8), slots(4)
    for j in range(1, 8):
        zt = add(z, j, 8)
        send(
            lambda zt=zt: JP.at[ym, zt], lambda: SD.at[kind_mine, zh], k_s + j,
            k_r + kind_mine * 2 + zh, dev(z_=zt), in_half,
        )

    @pl.when(in_half)
    def _():
        SD[kind_mine, zh] = JP[ym, z]

    recv(GMS, c_s)
    recv(XS, x_s)
    grad_sib = GMS[...]
    for kk in range(2):
        for zz in range(2):
            q = kk * 2 + zz
            part = pl.ds(zz * 4, 4)
            cg[q * C : (q + 1) * C, :] = dot(
                XB[2 * c + kk, part].reshape(N, C), grad_joined, 0, 0
            ) + dot(XS[kk, part].reshape(N, C), grad_sib, 0, 0)

    for kind in range(2):
        for zs in range(2):
            z_from = zs * 4 + kind * 2 + yq
            pl.when(z_from != z)(lambda: recv(SD.at[kind, zs], k_r + kind * 2 + zs))
    trunk_side = SD[0, 0].astype(f32) + SD[0, 1].astype(f32)
    embed_side = SD[1, 0].astype(f32) + SD[1, 1].astype(f32)
    trunk_normed = trunk * trunk_scale
    embed_normed = embed * embed_scale
    PRE[...] = GMF[zl] + trunk_scale * trunk_side
    SB4[:, 0:R] = to_rows(
        jnp.sum(trunk_side * trunk_normed, axis=1, keepdims=True),
        jnp.sum(embed_side * embed_normed, axis=1, keepdims=True),
    )
    s4_s, s4_r = slots(8), slots(8)
    for j in range(1, 8):
        send(lambda: SB4, lambda: SY4.at[y], s4_s + j, s4_r + y, dev(y_=add(y, j, 8)))
    SY4[y] = SB4[...]
    o_s, o_r = slots(4), slots(4)
    for j in range(1, 4):
        send(lambda: PRE, lambda: XPR.at[h], o_s + j, o_r + h, dev(h_=add(h, j, 4)))
    XPR[h] = PRE[...]

    for j in range(1, 4):
        hs = add(h, j, 4)
        recv(VR.at[hs], v_r + hs)
    vocab_total = jnp.sum(VR[...].astype(f32), axis=0)
    ug[...] = vocab_total
    VSB[...] = vocab_total.astype(bf16)
    q_s = slots(1)
    send(lambda: VSB, lambda: VSR, q_s, q_s, dev(z_=ozh * 4 + zl, c_=oc), donor)

    for j in range(1, 8):
        ys = add(y, j, 8)
        recv(SY4.at[ys], s4_r + ys)
    SB5[...] = jnp.sum(SY4[...], axis=0)
    s5_s, s5_r = slots(8), slots(8)
    for j in range(4):
        for flip in range(2):
            if j + flip:
                send(
                    lambda: SB5, lambda: S7.at[h, zh], s5_s + j * 2 + flip, s5_r + h * 2 + zh,
                    dev(h_=add(h, j, 4), z_=(ozh if flip else zh) * 4 + zl),
                )
    S7[h, zh] = SB5[...]
    for j in range(4):
        for flip in range(2):
            if j + flip:
                hs, zs = add(h, j, 4), (ozh if flip else zh)
                recv(S7.at[hs, zs], s5_r + hs * 2 + zs)
    every = jnp.sum(S7[...], axis=(0, 1))
    same = S7[h, 0] + S7[h, 1]
    ids = lax.broadcasted_iota(jnp.int32, (8, 128), 0)
    dots = to_cols(jnp.where(ids == 0, every, same)[:, 0:R])
    eg[...] = embed_scale * (embed_side - embed_normed * (pick(dots, 1) / D))
    for j in range(1, 4):
        hs = add(h, j, 4)
        recv(XPR.at[hs], o_r + hs)
    tg[...] = jnp.sum(XPR[...], axis=0) - trunk_scale * trunk_normed * (pick(dots, 0) / D)

    @pl.when(donor)
    def _():
        recv(VSR, q_s)
        ug[...] = VSR[...].astype(f32)

    for cond, body in finals:
        when(cond, body)


def local(
    trunk_hidden, next_embeds, combine_weight, final_gain, unembed_weight, target_ids, loss_scale
):
    core = lax.rem(lax.axis_index("dp"), 2)
    both = jnp.stack([trunk_hidden, next_embeds[0]])

    def mine(values):
        return lax.dynamic_index_in_dim(
            values.reshape(4, 2, R), core, axis=1, keepdims=False
        ).reshape(N, 1)

    vm = lambda *shape: pltpu.VMEM(shape, f32)
    vb = lambda *shape: pltpu.VMEM(shape, bf16)
    scratch = [
        vb(2, 1280, C), vb(4, 8, R, C), vb(2, 8, R, C), vm(4, R, CP), vm(4, R, CP), vm(R, CP),
        vb(8, R, CP), vm(4, R, C), vb(2, V, C), vm(8, N, VC), vm(8, N, VC), vm(4, R, 128),
        vb(2, N, C), vb(N, C),
        vm(8, VC), vm(8, 8, VC), vm(8, VC), vm(8, 8, VC), vm(8, VC), vm(8, 8, VC),
        vb(8, N, VC), vb(8, N, VC), vm(2, N, C), vb(8, R, C), vb(8, R, C),
        vm(4, R, CP), vm(R, 128), vm(4, R, 128), vm(8, VC), vm(8, 8, VC),
        vm(4, R, C), vb(N, C), vb(N, C), vb(4, 8, R, C), vb(4, 8, R, C), vb(2, 2, R, C),
        vm(R, C), vm(4, R, C), vm(8, 128), vm(8, 8, 128), vm(8, 128), vm(4, 2, 8, 128),
        vb(4, 512, C), vb(4, 512, C), vb(512, C), vb(512, C),
        pltpu.SemaphoreType.DMA((320,)), pltpu.SemaphoreType.DMA((320,)), pltpu.SemaphoreType.DMA((2,)),
    ]
    spec = pl.BlockSpec(memory_space=pltpu.VMEM)
    trunk_grad, embed_grad, combine_grad, unembed_grad = pl.pallas_call(
        kernel,
        out_shape=(
            jax.ShapeDtypeStruct((R, C), f32),
            jax.ShapeDtypeStruct((R, C), f32),
            jax.ShapeDtypeStruct((1280, C), f32),
            jax.ShapeDtypeStruct((512, C), f32),
        ),
        in_specs=[spec] * 6,
        out_specs=(spec,) * 4,
        scratch_shapes=scratch,
        compiler_params=pltpu.CompilerParams(
            collective_id=0, has_side_effects=True, vmem_limit_bytes=60 * 1024 * 1024
        ),
    )(
        both,
        combine_weight[0],
        unembed_weight,
        final_gain.reshape(1, C),
        mine(target_ids[0]),
        mine(loss_scale[0]),
    )
    return trunk_grad, embed_grad[None], combine_grad[None], unembed_grad[None, None]


def solution(mesh):
    in_specs = (
        P("dp", "tensor"),
        P("head", "dp", "tensor"),
        P("head", "dp", "tensor"),
        P("tensor"),
        P("dp", "tensor"),
        P("head", None),
        P("head", None),
    )
    out_specs = (
        P("dp", "tensor"),
        P("head", "dp", "tensor"),
        P("head", "dp", "tensor"),
        P("dp", "head", None, "tensor"),
    )
    return jax.shard_map(local, mesh=mesh, in_specs=in_specs, out_specs=out_specs, check_vma=False)
```

time: 1120 us -> 227 us (0.20)
  waiting for transfers between devices: 566 us -> 0 us
  blocking collectives: 472 us -> 0 us
  Pallas kernels: 0 us -> 207 us
  matrix products: 19.3 us -> 0 us
  other arithmetic: 18.7 us -> 2.84 us
  between operations: 14 us -> 0.67 us
  local copies, waits for them, and re-layouts: 25.4 us -> 13.1 us
    psum x1 -> x0, waiting for transfers between devices: 337 us -> none  [local(): logits = lax.psum(partial_logits, 'tensor')]
    all_gather x4 -> x0, blocking collectives: 283 us -> none  [the longest x1 157 us: local(): lax.all_gather(next_embeds[0], 'tensor', axis=1, tiled=True)]
    pallas_call x0 -> x1, Pallas kernels: none -> 207 us  [local(): pl.pallas_call(kernel, out_shape=(jax.ShapeDtypeStruct((R, C), f32), jax....]
    unnamed x6 -> x0, waiting for transfers between devices: 184 us -> none
    psum x5 -> x0, blocking collectives: 176 us -> none  [the longest x1 50.6 us: local(): mixed_sums = lax.psum(jnp.sum(mixed * mixed, axis=1), 'tensor')]
    reduce_scatter x2 -> x0, waiting for transfers between devices: 44.3 us -> none  [the longest x1 44.3 us: local(): lax.psum_scatter(jnp.dot(grad_local, unembed_weight, preferred_element_ty...]
    dot_general x6 -> x0, matrix products: 19.3 us -> none  [the longest x2 7.75 us: contract_cols(): lax.dot_general(left, right, (((1,), (1,)), ((), ())), preferred_element_...]
    pmax x1 -> x0, blocking collectives: 13.6 us -> none  [local(): largest = lax.pmax(jnp.max(logits, axis=1), 'dp')]
  transfers between devices with their start and end apart: 6 -> 0, of which waited for: 3 -> 0; matrix products, arithmetic and copies ran while one was open for 2% -> 0% of each run, Pallas kernels for 0% -> 0%
where the time goes in v1:
time: 227 us; the launch traced here: 223 us
  Pallas kernels  207 us (91%)
  local copies, waits for them, and re-layouts  13.1 us (6%)
  other arithmetic  2.84 us (1%)
    pallas_call x1, Pallas kernels, local(): pl.pallas_call(kernel, out_shape=(jax.ShapeDtypeStruct((R, C), f32), jax....  207 us
    unnamed x12, local copies, waits for them, and re-layouts  10 us

profile of v1, /device:TPU:56, one launch (start us, length us, event | category | flops | bytes accessed | tf_op | source)
XLA Modules:
  0.0 223.2 jit_solution(14335634507059572803)
XLA Ops:
  0.6 0.0 copy-start
  0.6 1.3 reshape.19.gain
  2.0 0.7 reduce
  2.7 0.1 reshape_squeeze.6
  2.8 0.7 reduce.1
  3.5 0.1 reshape_squeeze.7
  3.6 1.4 pad_maximum_fusion.xb
  5.0 0.7 reshape.23.wt
  5.8 0.8 reshape.22.tgt
  6.5 2.2 copy.17
  8.8 0.0 copy-done
  8.8 1.5 copy.20.u
  10.3 206.6 %shard_map.102 = (f32[48,320]{1,0:T(8,128)}, f32[48,320]{1,0:T(8,128)}, f32[1280,320]{1,0:T(8,128)}, f32[512,320]{1,0:T(8,128)}) custom-call(bf16[2,48,320]{2,1,0:T(8,128)(2,1)} %pad_maximum_fusion.xb, bf16[1280,320]{1,0:T(8,128)(2,1)} %bitcast.11, bf16[2048,320]{1,0:T(8,128)(2,1)} %copy.20.u, f32[1,320]{1,0:T(1,128)} %reshape.19.gain, ...), custom_call_target="tpu_custom_call" | custom-call | tf_op jit(solution)/shard_map/pallas_call | solution.py:578
  216.9 2.2 copy.24
  219.2 0.0 copy-start.2
  219.2 0.0 copy-start.1
  219.2 2.8 %copy.23 = f32[1,1280,320]{1,2,0:T(8,128)} copy(f32[1,1280,320]{2,1,0:T(8,128)} %bitcast.12) | data formatting | bytes 3276800
  221.9 0.0 copy-done.2
  221.9 0.6 copy.29
  222.6 0.0 copy-done.1
  222.6 0.6 copy.30
  (2 shorter events, 0.0 us)
Async XLA Ops:
  0.6 8.1 %copy-start = (bf16[2048,320]{0,1:T(8,128)(2,1)S(1)}, bf16[2048,320]{0,1:T(8,128)(2,1)}, u32[]{:S(2)}) copy-start(bf16[2048,320]{0,1:T(8,128)(2,1)} %param.11) | copy-start | bytes 3932164
  219.2 2.8 %copy-start.2 = (f32[48,320]{1,0:T(8,128)S(1)}, f32[48,320]{1,0:T(8,128)}, u32[]{:S(2)}) copy-start(f32[48,320]{1,0:T(8,128)} %get-tuple-element.24) | copy-start | bytes 184324
  219.2 3.4 %copy-start.1 = (f32[48,320]{1,0:T(8,128)S(1)}, f32[48,320]{1,0:T(8,128)}, u32[]{:S(2)}) copy-start(f32[48,320]{1,0:T(8,128)} %get-tuple-element.9) | copy-start | bytes 184324

commit v2 on v1

--- a/solution.py
+++ b/solution.py
@@ -15,6 +15,8 @@
 VC = 256
 MESH = pl.DeviceIdType.MESH
 HI = lax.Precision.HIGHEST
+PAIRS = 128
+SEMS = 256
 f32 = jnp.float32
 bf16 = jnp.bfloat16
 
@@ -26,10 +28,11 @@
 
 
 def kernel(
-    xb, w, u, gain, tgt, wt,
+    trunk_in, embed_in, w, u, gain, ids_in, scale_in,
+    tg_out, eg_out, cg_out, ug_out,
     tg, eg, cg, ug,
     W2, XB, XS, PB, R2, T, Y8, MX, UP, LP, RL, MSC, YN, YS,
-    SB0, SY0, SB1, SY1, SB2, SZ2, GA, GS, GN, NB, NR, SG, DCB, DCR, SB3, SY3,
+    SB0, SY0, SB1, SY1, SB2, SZ2, GA, GS, GN, NB, NR, SG, DCB, DCR, SB3, SY3, RL2, TW,
     GMF, GML, GMS, JP, RJ, SD, PRE, XPR, SB4, SY4, SB5, S7, VB, VR, VSB, VSR,
     ssem, rsem, lsem,
 ):
@@ -55,12 +58,15 @@
     right, left = dev(y_=add(y, 1, 8)), dev(y_=add(y, -1, 8))
     me = dev()
 
-    counts = {"s": 0, "r": 0}
-
-    def slots(n):
-        first = counts["s"]
-        counts["s"] += n
+    counts = {"both": 0, "s": PAIRS, "r": PAIRS}
+
+    def slots(n, which="both"):
+        first = counts[which]
+        counts[which] += n
         return first
+
+    def some(sends, receives):
+        return slots(sends, "s"), slots(receives, "r")
 
     finals = []
 
@@ -82,6 +88,10 @@
 
     def recv(dst, r):
         copy(dst, dst, 0, r, me).wait_recv()
+
+    def put(at):
+        pairs = ((tg, tg_out), (eg, eg_out), (cg, cg_out), (ug, ug_out))
+        return pltpu.make_async_copy(*pairs[at], lsem.at[2 + at])
 
     lane = lax.broadcasted_iota(jnp.int32, (R, CP), 1)
     e8 = (
@@ -117,25 +127,31 @@
     own_w = pltpu.make_async_copy(w, W2.at[c], lsem.at[0])
     own_w.start()
     T[...] = jnp.zeros_like(T)
-    for ref in (SB0, SB1, SB2, SB3, SB4, SB5):
+    for ref in (SB0, SB1, SB2, SB3, SB4, SB5, DCB):
         ref[...] = jnp.zeros_like(ref)
     PB[...] = jnp.zeros_like(PB)
+    two = lax.broadcasted_iota(jnp.int32, (8, 384), 0)
+    TW[...] = to_cols(
+        jnp.where(two == 0, ids_in[...].astype(f32), jnp.where(two == 1, scale_in[...], 0.0))
+    ).reshape(4, 2, R, 128)
+    chosen = jnp.concatenate([TW[j, c] for j in range(4)], axis=0)
+    targets, weights = pick(chosen, 0), pick(chosen, 1)
     pl.semaphore_wait(barrier, len(peers))
 
     yq, ym = lax.div(y, 4), lax.rem(y, 4)
     hf = lax.rem(zl, 2)
     in_half = hf == yq
-    a_s, a_r = slots(4), slots(8)
+    a_s, a_r = some(4, 8)
     for kind in range(2):
         for zh_to in range(2):
             z_to = zh_to * 4 + kind * 2 + yq
             send(
-                lambda kind=kind: xb.at[kind], lambda: XB.at[ym, z],
+                lambda kind=kind: (trunk_in, embed_in)[kind], lambda: XB.at[ym, z],
                 a_s + kind * 2 + zh_to, a_r + z, dev(z_=z_to), z_to != z,
             )
 
             def keep(kind=kind):
-                XB[ym, z] = xb[kind]
+                XB[ym, z] = (trunk_in, embed_in)[kind][...]
 
             pl.when(z_to == z)(keep)
     w_s = slots(1)
@@ -143,44 +159,48 @@
 
     owner = c == zh
     donor = c != zh
-    u_q, u_f, u_x, u_d, u_b = slots(4), slots(1), slots(4), slots(1), slots(4)
+    u_f = slots(1)
+    u_x, u_q = some(9, 4)
+    u_b, u_d = u_x + 4, u_x + 8
     own_u = lambda: pltpu.make_async_copy(u, UP.at[zh], lsem.at[1])
     pl.when(owner)(lambda: own_u().start())
 
-    @pl.when(in_half)
-    def _():
-        for j in range(1, 8):
-            zs = add(z, j, 8)
-            recv(XB.at[ym, zs], a_r + zs)
-
-    mine = pl.ds(h * 512, 512)
-    send(lambda: u.at[mine], lambda: UP.at[zh, mine], u_d, u_q + h, dev(z_=ozh * 4 + zl), donor)
-
-    b_s = slots(16)
+    def quarter_of(at):
+        return pl.ds(pl.multiple_of(at * 512, 512), 512)
+
+    mine = quarter_of(h)
+    b_s = slots(32)
     for i in range(8):
-        for way in range(2):
-            s = add(y, -i, 8) if way == 0 else add(y, i, 8)
-            k = lax.rem(s, 4)
-            cond = lax.div(s, 4) == hf
-            for unit in range(2):
-                part = pl.ds(way * 4 + unit * 2, 2)
-                idx = b_s + (way * 4 + k) * 2 + unit
-                if i > 0:
-                    pl.when(cond)(lambda: recv(XB.at[k, part], idx))
+        for unit in range(4):
+            for way in range(2):
+                s = add(y, -i, 8) if way == 0 else add(y, i, 8)
+                k = lax.rem(s, 4)
+                cond = lax.div(s, 4) == hf
+                zs = way * 4 + unit
+                idx = b_s + k * 8 + zs
+                if i == 0:
+                    pl.when(in_half & (z != zs))(lambda: recv(XB.at[ym, zs], a_r + zs))
+                else:
+                    pl.when(cond)(lambda: recv(XB.at[k, zs], idx))
                 if i < 7:
                     send(
-                        lambda k=k, part=part: XB.at[k, part], lambda k=k, part=part: XB.at[k, part],
+                        lambda k=k, zs=zs: XB.at[k, zs], lambda k=k, zs=zs: XB.at[k, zs],
                         idx, idx, right if way == 0 else left, cond,
                     )
+        if i == 1:
+            send(
+                lambda: u.at[:, mine], lambda: UP.at[zh, :, mine], u_d, u_q + h,
+                dev(z_=ozh * 4 + zl), donor,
+            )
 
     send(lambda: u, lambda: UP.at[zh], u_f, u_f, sib, owner)
-    pl.when(owner)(lambda: recv(UP.at[ozh, mine], u_q + h))
+    pl.when(owner)(lambda: recv(UP.at[ozh, :, mine], u_q + h))
     for j in range(1, 4):
         send(
-            lambda: UP.at[ozh, mine], lambda: UP.at[ozh, mine], u_x + j, u_q + h,
+            lambda: UP.at[ozh, :, mine], lambda: UP.at[ozh, :, mine], u_x + j, u_q + h,
             dev(h_=add(h, j, 4)), owner,
         )
-    send(lambda: UP.at[ozh, mine], lambda: UP.at[ozh, mine], u_b, u_q + h, sib, owner)
+    send(lambda: UP.at[ozh, :, mine], lambda: UP.at[ozh, :, mine], u_b, u_q + h, sib, owner)
 
     own_w.wait()
     recv(W2.at[oc], w_s)
@@ -188,13 +208,13 @@
     squares = jnp.zeros((N, 1), f32)
     for q in range(8):
         block = XB[q // 2, (q % 2) * 4 : (q % 2) * 4 + 4].reshape(N, C)
-        acc = acc + dot(block, W2[q // 4, (q % 4) * C : (q % 4 + 1) * C, :], 1, 0)
+        acc = acc + dot(block, W2[q // 4, :, (q % 4) * C : (q % 4 + 1) * C], 1, 1)
         wide = block.astype(f32)
         squares = squares + jnp.sum(wide * wide, axis=1, keepdims=True)
     PB[:, :, 0:C] = acc.reshape(4, R, C)
     lane3 = lax.broadcasted_iota(jnp.int32, (4, R, CP), 2)
     PB[...] = jnp.where(lane3 >= C, squares.reshape(4, R, 1), PB[...])
-    p_s, p_r = slots(4), slots(4)
+    p_s, p_r = some(4, 4)
     for j in range(1, 4):
         zt = add(zl, j, 4)
         send(
@@ -208,38 +228,38 @@
         recv(R2.at[zt], p_r + zt)
     from_trunk = R2[0] + R2[1]
     from_embed = R2[2] + R2[3]
-    trunk = xb[0].astype(f32)
-    embed = xb[1].astype(f32)
+    trunk = trunk_in[...].astype(f32)
+    embed = embed_in[...].astype(f32)
     trunk_scale = lax.rsqrt(pick(from_trunk, C) / D + EPS)
     embed_scale = lax.rsqrt(pick(from_embed, C) / D + EPS)
     mixed = trunk + trunk_scale * from_trunk[:, 0:C] + embed_scale * from_embed[:, 0:C]
     MX[zl] = mixed
-    gains = gain[...]
+    gains = gain[...].reshape(1, C)
     total = jnp.sum(mixed * mixed, axis=1, keepdims=True)
     high = total.astype(bf16).astype(f32)
     middle = (total - high).astype(bf16).astype(f32)
     low = total - high - middle
     pieces = jnp.where(lane == C, high, jnp.where(lane == C + 1, middle, low))
     Y8[z] = widen(mixed * gains, pieces).astype(bf16)
-    y_s, y_r = slots(8), slots(8)
+    y_s, y_r = some(8, 8)
     for j in range(1, 8):
         send(lambda: Y8.at[z], lambda: Y8.at[z], y_s + j, y_r + z, dev(z_=add(z, j, 8)))
-    m_s, m_r = slots(4), slots(4)
+    for j in range(1, 4):
+        ht = add(h, j, 4)
+        quarter = quarter_of(ht)
+        pl.when(owner)(lambda: recv(UP.at[ozh, :, quarter], u_q + ht))
+        send(
+            lambda quarter=quarter: UP.at[ozh, :, quarter], lambda quarter=quarter: UP.at[ozh, :, quarter],
+            u_b + j, u_q + ht, sib, owner,
+        )
+    for j in range(1, 8):
+        zs = add(z, j, 8)
+        recv(Y8.at[zs], y_r + zs)
+    m_s, m_r = some(4, 4)
     for j in range(1, 4):
         send(
             lambda: MX.at[zl], lambda: MX.at[zl], m_s + j, m_r + zl, dev(z_=zh * 4 + add(zl, j, 4))
         )
-    for j in range(1, 4):
-        ht = add(h, j, 4)
-        quarter = pl.ds(ht * 512, 512)
-        pl.when(owner)(lambda: recv(UP.at[ozh, quarter], u_q + ht))
-        send(
-            lambda quarter=quarter: UP.at[ozh, quarter], lambda quarter=quarter: UP.at[ozh, quarter],
-            u_b + j, u_q + ht, sib, owner,
-        )
-    for j in range(1, 8):
-        zs = add(z, j, 8)
-        recv(Y8.at[zs], y_r + zs)
 
     wide = Y8[...].astype(f32)
     ids = lax.broadcasted_iota(jnp.int32, wide.shape, 2)
@@ -248,7 +268,7 @@
     )
     part_squares = (split[0:4] + split[4:8]).reshape(N, 1)
     SB0[:, 0:N] = to_rows(part_squares)
-    s0_s, s0_r = slots(8), slots(8)
+    s0_s, s0_r = some(8, 8)
     for j in range(1, 8):
         send(lambda: SB0, lambda: SY0.at[y], s0_s + j, s0_r + y, dev(y_=add(y, j, 8)))
     SY0[y] = SB0[...]
@@ -261,33 +281,53 @@
     def _():
         recv(UP.at[zh], u_f)
         for j in range(4):
-            recv(UP.at[ozh, pl.ds(j * 512, 512)], u_q + j)
+            recv(UP.at[ozh, :, pl.ds(j * 512, 512)], u_q + j)
 
     y0 = Y8[0:4].reshape(N, CP)[:, 0:C]
     y1 = Y8[4:8].reshape(N, CP)[:, 0:C]
 
-    def logits_block(at, carry):
-        rows = pl.ds(pl.multiple_of(at * VC, VC), VC)
-        LP[at] = dot(y0, UP[0, rows, :], 1, 1) + dot(y1, UP[1, rows, :], 1, 1)
-        return carry
-
-    lax.fori_loop(0, 8, logits_block, 0)
+    def logits_block(at):
+        cols = pl.ds(pl.multiple_of(at * VC, VC), VC)
+        LP[at] = dot(y0, UP[0, :, cols], 1, 0) + dot(y1, UP[1, :, cols], 1, 0)
+
     l_s = slots(32)
-    for i in range(8):
-        for way in range(2):
-            to = add(y, -1 - i, 8) if way == 0 else add(y, 1 + i, 8)
-            for unit in range(2):
-                rows = slice(way * 96 + unit * 48, way * 96 + unit * 48 + 48)
-                idx = l_s + (way * 8 + i) * 2 + unit
-                if i > 0:
-                    recv(RL.at[to, rows], idx - 2)
-                    LP[to, rows] = LP[to, rows] + RL[to, rows]
-                if i < 7:
-                    send(
-                        lambda to=to, rows=rows: LP.at[to, rows],
-                        lambda to=to, rows=rows: RL.at[to, rows],
-                        idx, idx, right if way == 0 else left,
-                    )
+
+    def hop(o, way, unit, got):
+        to = add(y, o, 8) if way == 0 else add(y, -o, 8)
+        rows = slice(unit * R, unit * R + R)
+        idx = l_s + (way * 4 + o) * 4 + unit
+        if got:
+            last = RL2 if (o == 0 and way == 1) else RL.at[to]
+            recv(last.at[rows], idx)
+            LP[to, rows] = LP[to, rows] + last[rows]
+        if o:
+            place = RL2 if (o == 1 and way == 1) else RL.at[to]
+            send(
+                lambda: LP.at[to, rows], lambda: place.at[rows], idx - 4, idx - 4,
+                right if way == 0 else left,
+            )
+
+    logits_block(add(y, 4, 8))
+    for unit in range(2):
+        hop(4, 0, unit, False)
+        hop(4, 1, unit + 2, False)
+    logits_block(add(y, 3, 8))
+    logits_block(add(y, -3, 8))
+    for unit in range(2):
+        hop(3, 0, unit + 2, False)
+        hop(3, 1, unit, False)
+    logits_block(add(y, 2, 8))
+    logits_block(add(y, -2, 8))
+    for unit in range(2):
+        hop(3, 0, unit, True)
+        hop(3, 1, unit + 2, True)
+    logits_block(add(y, 1, 8))
+    logits_block(add(y, -1, 8))
+    logits_block(y)
+    for o in (2, 1, 0):
+        for unit in (2, 3, 0, 1):
+            hop(o, 0, unit, True)
+            hop(o, 1, (unit + 2) % 4, True)
     for j in range(1, 8):
         ys = add(y, j, 8)
         recv(SY0.at[ys], s0_r + ys)
@@ -303,7 +343,7 @@
     largest = jnp.max(logits, axis=1, keepdims=True)
     summed = jnp.sum(jnp.exp(logits - largest), axis=1, keepdims=True)
     SB1[:, 0:N] = to_rows(largest, summed)
-    s1_s, s1_r = slots(8), slots(8)
+    s1_s, s1_r = some(8, 8)
     for j in range(1, 8):
         send(lambda: SB1, lambda: SY1.at[y], s1_s + j, s1_r + y, dev(y_=add(y, j, 8)))
     SY1[y] = SB1[...]
@@ -319,7 +359,7 @@
         ys = add(y, j, 8)
         recv(SY1.at[ys], s1_r + ys)
     SB2[...] = merge(SY1)
-    s2_s, s2_r = slots(8), slots(8)
+    s2_s, s2_r = some(8, 8)
     for j in range(1, 8):
         send(lambda: SB2, lambda: SZ2.at[z], s2_s + j, s2_r + z, dev(z_=add(z, j, 8)))
     SZ2[z] = SB2[...]
@@ -329,8 +369,8 @@
     stats = to_cols(merge(SZ2)[:, 0:N])
     probs = jnp.exp(logits - pick(stats, 0)) / pick(stats, 1)
     vocab_ids = (zl * 4096 + zh * 2048 + y * VC) + lax.broadcasted_iota(jnp.int32, (N, VC), 1)
-    hits = (vocab_ids == tgt[...]).astype(f32)
-    GA[y] = (wt[...] * (probs - hits)).astype(bf16)
+    hits = (vocab_ids.astype(f32) == targets).astype(f32)
+    GA[y] = (weights * (probs - hits)).astype(bf16)
 
     g_s = slots(20)
     for i in range(5):
@@ -355,33 +395,16 @@
         rows = pl.ds(pl.multiple_of(at * VC, VC), VC)
         grads = GA[at]
         for zc in range(2):
-            GN[zc] += dot(grads, UP[zc, rows, :], 1, 0)
+            GN[zc] += dot(grads, UP[zc, :, rows], 1, 1)
         return carry
 
     lax.fori_loop(0, 8, normed_block, 0)
     NB[...] = GN[...].astype(bf16).reshape(8, R, C)
-    n8_s, n8_r = slots(8), slots(8)
+    n8_s, n8_r = some(8, 8)
     for j in range(1, 8):
         zt = add(z, j, 8)
         send(lambda zt=zt: NB.at[zt], lambda: NR.at[z], n8_s + j, n8_r + z, dev(z_=zt))
     NR[z] = NB[z]
-
-    recv(GS, gs_s)
-    recv(YS, n_s)
-    normed_mine = YN[c]
-    normed_sib = YS[...]
-
-    def vocab_block(at, carry):
-        value = dot(GA[at], normed_mine, 0, 0) + dot(GS[at], normed_sib, 0, 0)
-        VB[lax.div(at, 2), pl.ds(pl.multiple_of(lax.rem(at, 2) * VC, VC), VC), :] = value.astype(bf16)
-        return carry
-
-    lax.fori_loop(0, 8, vocab_block, 0)
-    v_s, v_r = slots(4), slots(4)
-    for j in range(1, 4):
-        ht = add(h, j, 4)
-        send(lambda ht=ht: VB.at[ht], lambda: VR.at[h], v_s + j, v_r + h, dev(h_=ht))
-    VR[h] = VB[h]
 
     for j in range(1, 8):
         zs = add(z, j, 8)
@@ -395,23 +418,42 @@
     SG[zl] = widen(
         scaled, jnp.where(lane == C, inner, jnp.where(lane == C + 1, trunk_scale, embed_scale))
     )
-    DCB[...] = jnp.broadcast_to(inner, (R, 128))
-    d_s, d_r, e_s, e_r = slots(4), slots(4), slots(4), slots(4)
+    DCB[:, 0:R] = to_rows(inner)
+    d_s, d_r = some(4, 4)
+    e_s, e_r = some(4, 4)
     for j in range(1, 4):
         zt = add(zl, j, 4)
         send(lambda: SG.at[zl], lambda: SG.at[zl], d_s + j, d_r + zl, dev(z_=zh * 4 + zt))
     for j in range(4):
         zt = add(zl, j, 4)
         send(lambda: DCB, lambda: DCR.at[zl], e_s + j, e_r + zl, dev(z_=ozh * 4 + zt))
+    recv(GS, gs_s)
+    recv(YS, n_s)
+    normed_mine = YN[c]
+    normed_sib = YS[...]
+
+    def vocab_block(at, carry):
+        value = dot(normed_mine, GA[at], 0, 0) + dot(normed_sib, GS[at], 0, 0)
+        VB[lax.div(at, 2), :, pl.ds(pl.multiple_of(lax.rem(at, 2) * VC, VC), VC)] = value.astype(bf16)
+        return carry
+
+    lax.fori_loop(0, 8, vocab_block, 0)
+    v_s, v_r = some(4, 4)
+    for j in range(1, 4):
+        ht = add(h, j, 4)
+        send(lambda ht=ht: VB.at[ht], lambda: VR.at[h], v_s + j, v_r + h, dev(h_=ht))
+    VR[h] = VB[h]
+
     for j in range(1, 4):
         zs = add(zl, j, 4)
         recv(SG.at[zs], d_r + zs)
     for j in range(4):
         zs = add(zl, j, 4)
         recv(DCR.at[zs], e_r + zs)
-    inner_part = (pick(SG[...], C) + pick(DCR[...], 0)).reshape(N, 1)
+    other = jnp.concatenate([to_cols(DCR[j][:, 0:R]) for j in range(4)], axis=0)
+    inner_part = pick(SG[...], C).reshape(N, 1) + pick(other, 0)
     SB3[:, 0:N] = to_rows(inner_part)
-    s3_s, s3_r = slots(8), slots(8)
+    s3_s, s3_r = some(8, 8)
     for j in range(1, 8):
         send(lambda: SB3, lambda: SY3.at[y], s3_s + j, s3_r + y, dev(y_=add(y, j, 8)))
     SY3[y] = SB3[...]
@@ -434,17 +476,28 @@
     send(lambda: GML, lambda: GMS, c_s, c_s, sib)
 
     for q in range(8):
-        value = dot(grad_low, W2[q // 4, (q % 4) * C : (q % 4 + 1) * C, :], 1, 1)
+        value = dot(grad_low, W2[q // 4, :, (q % 4) * C : (q % 4 + 1) * C], 1, 0)
         JP[q // 2, (q % 2) * 4 : (q % 2) * 4 + 4] = value.astype(bf16).reshape(4, R, C)
-    j_s = slots(16)
+    q_s = slots(1)
+
+    def sum_vocab():
+        for j in range(1, 4):
+            hs = add(h, j, 4)
+            recv(VR.at[hs], v_r + hs)
+        vocab_total = jnp.sum(VR[...].astype(f32), axis=0)
+        ug[...] = vocab_total
+        VSB[...] = vocab_total.astype(bf16)
+        send(lambda: VSB, lambda: VSR, q_s, q_s, dev(z_=ozh * 4 + zl, c_=oc), donor)
+
+    j_s = slots(32)
     for i in range(8):
-        for way in range(2):
-            to = add(y, -1 - i, 8) if way == 0 else add(y, 1 + i, 8)
-            k = lax.rem(to, 4)
-            cond = lax.div(to, 4) == hf
-            for unit in range(2):
-                part = pl.ds(way * 4 + unit * 2, 2)
-                idx = j_s + (way * 4 + k) * 2 + unit
+        for unit in range(4):
+            for way in range(2):
+                to = add(y, -1 - i, 8) if way == 0 else add(y, 1 + i, 8)
+                k = lax.rem(to, 4)
+                cond = lax.div(to, 4) == hf
+                part = way * 4 + unit
+                idx = j_s + k * 8 + part
 
                 def take():
                     recv(RJ.at[k, part], idx)
@@ -457,8 +510,10 @@
                         lambda k=k, part=part: JP.at[k, part], lambda k=k, part=part: RJ.at[k, part],
                         idx, idx, right if way == 0 else left, cond,
                     )
+        if i == 0:
+            sum_vocab()
     kind_mine = lax.div(zl, 2)
-    k_s, k_r = slots(8), slots(4)
+    k_s, k_r = some(8, 4)
     for j in range(1, 8):
         zt = add(z, j, 8)
         send(
@@ -477,10 +532,11 @@
         for zz in range(2):
             q = kk * 2 + zz
             part = pl.ds(zz * 4, 4)
-            cg[q * C : (q + 1) * C, :] = dot(
-                XB[2 * c + kk, part].reshape(N, C), grad_joined, 0, 0
-            ) + dot(XS[kk, part].reshape(N, C), grad_sib, 0, 0)
-
+            cg[:, q * C : (q + 1) * C] = dot(
+                grad_joined, XB[2 * c + kk, part].reshape(N, C), 0, 0
+            ) + dot(grad_sib, XS[kk, part].reshape(N, C), 0, 0)
+
+    put(2).start()
     for kind in range(2):
         for zs in range(2):
             z_from = zs * 4 + kind * 2 + yq
@@ -494,29 +550,20 @@
         jnp.sum(trunk_side * trunk_normed, axis=1, keepdims=True),
         jnp.sum(embed_side * embed_normed, axis=1, keepdims=True),
     )
-    s4_s, s4_r = slots(8), slots(8)
+    s4_s, s4_r = some(8, 8)
     for j in range(1, 8):
         send(lambda: SB4, lambda: SY4.at[y], s4_s + j, s4_r + y, dev(y_=add(y, j, 8)))
     SY4[y] = SB4[...]
-    o_s, o_r = slots(4), slots(4)
+    o_s, o_r = some(4, 4)
     for j in range(1, 4):
         send(lambda: PRE, lambda: XPR.at[h], o_s + j, o_r + h, dev(h_=add(h, j, 4)))
     XPR[h] = PRE[...]
-
-    for j in range(1, 4):
-        hs = add(h, j, 4)
-        recv(VR.at[hs], v_r + hs)
-    vocab_total = jnp.sum(VR[...].astype(f32), axis=0)
-    ug[...] = vocab_total
-    VSB[...] = vocab_total.astype(bf16)
-    q_s = slots(1)
-    send(lambda: VSB, lambda: VSR, q_s, q_s, dev(z_=ozh * 4 + zl, c_=oc), donor)
 
     for j in range(1, 8):
         ys = add(y, j, 8)
         recv(SY4.at[ys], s4_r + ys)
     SB5[...] = jnp.sum(SY4[...], axis=0)
-    s5_s, s5_r = slots(8), slots(8)
+    s5_s, s5_r = some(8, 8)
     for j in range(4):
         for flip in range(2):
             if j + flip:
@@ -534,70 +581,98 @@
     same = S7[h, 0] + S7[h, 1]
     ids = lax.broadcasted_iota(jnp.int32, (8, 128), 0)
     dots = to_cols(jnp.where(ids == 0, every, same)[:, 0:R])
+    pl.when(owner)(lambda: put(3).start())
     eg[...] = embed_scale * (embed_side - embed_normed * (pick(dots, 1) / D))
+    put(1).start()
     for j in range(1, 4):
         hs = add(h, j, 4)
         recv(XPR.at[hs], o_r + hs)
     tg[...] = jnp.sum(XPR[...], axis=0) - trunk_scale * trunk_normed * (pick(dots, 0) / D)
+
+    put(0).start()
 
     @pl.when(donor)
     def _():
         recv(VSR, q_s)
         ug[...] = VSR[...].astype(f32)
-
+        put(3).start()
+
+    for at in range(4):
+        put(at).wait()
+    assert counts["both"] <= PAIRS and max(counts.values()) <= SEMS
     for cond, body in finals:
         when(cond, body)
+
+
+def put_out(*refs):
+    into, out, held, sems = refs[:4], refs[4:8], refs[8:12], refs[12]
+    reads = [pltpu.make_async_copy(into[k], held[k], sems.at[k]) for k in range(4)]
+    writes = [pltpu.make_async_copy(held[k], out[k], sems.at[k + 4]) for k in range(4)]
+    order = (2, 3, 0, 1)
+    for k in order:
+        reads[k].start()
+    for k in order:
+        reads[k].wait()
+        writes[k].start()
+    for k in order:
+        writes[k].wait()
 
 
 def local(
     trunk_hidden, next_embeds, combine_weight, final_gain, unembed_weight, target_ids, loss_scale
 ):
-    core = lax.rem(lax.axis_index("dp"), 2)
-    both = jnp.stack([trunk_hidden, next_embeds[0]])
-
-    def mine(values):
-        return lax.dynamic_index_in_dim(
-            values.reshape(4, 2, R), core, axis=1, keepdims=False
-        ).reshape(N, 1)
-
     vm = lambda *shape: pltpu.VMEM(shape, f32)
     vb = lambda *shape: pltpu.VMEM(shape, bf16)
     scratch = [
-        vb(2, 1280, C), vb(4, 8, R, C), vb(2, 8, R, C), vm(4, R, CP), vm(4, R, CP), vm(R, CP),
-        vb(8, R, CP), vm(4, R, C), vb(2, V, C), vm(8, N, VC), vm(8, N, VC), vm(4, R, 128),
+        vm(R, C), vm(R, C), vm(C, 1280), vm(C, 512),
+        vb(2, C, 1280), vb(4, 8, R, C), vb(2, 8, R, C), vm(4, R, CP), vm(4, R, CP), vm(R, CP),
+        vb(8, R, CP), vm(4, R, C), vb(2, C, V), vm(8, N, VC), vm(8, N, VC), vm(4, R, 128),
         vb(2, N, C), vb(N, C),
         vm(8, VC), vm(8, 8, VC), vm(8, VC), vm(8, 8, VC), vm(8, VC), vm(8, 8, VC),
         vb(8, N, VC), vb(8, N, VC), vm(2, N, C), vb(8, R, C), vb(8, R, C),
-        vm(4, R, CP), vm(R, 128), vm(4, R, 128), vm(8, VC), vm(8, 8, VC),
+        vm(4, R, CP), vm(8, 128), vm(4, 8, 128), vm(8, VC), vm(8, 8, VC),
+        vm(N, VC), vm(4, 2, R, 128),
         vm(4, R, C), vb(N, C), vb(N, C), vb(4, 8, R, C), vb(4, 8, R, C), vb(2, 2, R, C),
         vm(R, C), vm(4, R, C), vm(8, 128), vm(8, 8, 128), vm(8, 128), vm(4, 2, 8, 128),
-        vb(4, 512, C), vb(4, 512, C), vb(512, C), vb(512, C),
-        pltpu.SemaphoreType.DMA((320,)), pltpu.SemaphoreType.DMA((320,)), pltpu.SemaphoreType.DMA((2,)),
+        vb(4, C, 512), vb(4, C, 512), vb(C, 512), vb(C, 512),
+        pltpu.SemaphoreType.DMA((SEMS,)), pltpu.SemaphoreType.DMA((SEMS,)), pltpu.SemaphoreType.DMA((6,)),
     ]
     spec = pl.BlockSpec(memory_space=pltpu.VMEM)
+    remote = pl.BlockSpec(memory_space=pl.ANY)
     trunk_grad, embed_grad, combine_grad, unembed_grad = pl.pallas_call(
         kernel,
         out_shape=(
             jax.ShapeDtypeStruct((R, C), f32),
             jax.ShapeDtypeStruct((R, C), f32),
-            jax.ShapeDtypeStruct((1280, C), f32),
-            jax.ShapeDtypeStruct((512, C), f32),
+            jax.ShapeDtypeStruct((C, 1280), f32),
+            jax.ShapeDtypeStruct((C, 512), f32),
         ),
-        in_specs=[spec] * 6,
-        out_specs=(spec,) * 4,
+        in_specs=[spec, spec, remote, remote, spec, spec, spec],
+        out_specs=(remote,) * 4,
         scratch_shapes=scratch,
         compiler_params=pltpu.CompilerParams(
             collective_id=0, has_side_effects=True, vmem_limit_bytes=60 * 1024 * 1024
         ),
     )(
-        both,
-        combine_weight[0],
-        unembed_weight,
-        final_gain.reshape(1, C),
-        mine(target_ids[0]),
-        mine(loss_scale[0]),
-    )
-    return trunk_grad, embed_grad[None], combine_grad[None], unembed_grad[None, None]
+        trunk_hidden,
+        next_embeds[0],
+        combine_weight[0].T,
+        unembed_weight.T,
+        final_gain,
+        target_ids,
+        loss_scale,
+    )
+    results = (trunk_grad, embed_grad, combine_grad, unembed_grad)
+    trunk_grad, embed_grad, combine_grad, unembed_grad = pl.pallas_call(
+        put_out,
+        out_shape=tuple(jax.ShapeDtypeStruct(r.shape, r.dtype) for r in results),
+        in_specs=[remote] * 4,
+        out_specs=(remote,) * 4,
+        scratch_shapes=[pltpu.VMEM(r.shape, r.dtype) for r in results]
+        + [pltpu.SemaphoreType.DMA((8,))],
+        compiler_params=pltpu.CompilerParams(vmem_limit_bytes=60 * 1024 * 1024),
+    )(*results)
+    return trunk_grad, embed_grad[None], combine_grad.T[None], unembed_grad.T[None, None]
 
 
 def solution(mesh):

time: 227 us -> 182 us (0.80); the launches traced: 223 us -> 182 us
  Pallas kernels: 207 us -> 181 us
  local copies, waits for them, and re-layouts: 13.1 us -> 0 us
  other arithmetic: 2.84 us -> 0 us
    pallas_call x1, Pallas kernels: 207 us -> 178 us  [local(): pl.pallas_call(kernel, out_shape=(jax.ShapeDtypeStruct((R, C), f32), jax....]
    unnamed x12 -> x0, local copies, waits for them, and re-layouts: 10 us -> none
    pallas_call x0 -> x1, Pallas kernels: none -> 2.91 us  [local(): pl.pallas_call(put_out, out_shape=tuple((jax.ShapeDtypeStruct(r.shape, r....]
    reshape x3 -> x0, local copies, waits for them, and re-layouts: 2.86 us -> none  [the longest x2 1.51 us: mine(): return lax.dynamic_index_in_dim(values.reshape(4, 2, R), core, axis=1, ke...]
where the time goes in v2:
time: 182 us
  Pallas kernels  181 us (99%)
    pallas_call x1, Pallas kernels, local(): pl.pallas_call(kernel, out_shape=(jax.ShapeDtypeStruct((R, C), f32), jax....  178 us

profile of v2, /device:TPU:56, one launch (start us, length us, event | category | flops | bytes accessed | tf_op | source)
XLA Modules:
  0.0 182.0 jit_solution(15382155159678791456)
XLA Ops:
  0.6 178.4 %shard_map.102 = (f32[48,320]{1,0:T(8,128)}, f32[48,320]{1,0:T(8,128)}, f32[320,1280]{1,0:T(8,128)}, f32[320,512]{1,0:T(8,128)}) custom-call(bf16[48,320]{1,0:T(8,128)(2,1)} %trunk_in.1, bf16[48,320]{1,0:T(8,128)(2,1)} %bitcast.14, bf16[320,1280]{1,0:T(8,128)(2,1)} %bitcast.13, bf16[320,2048]{1,0:T(8,128)(2,1)} %bitcast.12, f32[320]{0:T(512)} %gain.1, ...), custom_call_target="tpu_custom_call" | custom-call | tf_op jit(solution)/shard_map/pallas_call | solution.py:642
  179.1 2.9 %shard_map.103 = (f32[48,320]{1,0:T(8,128)}, f32[48,320]{1,0:T(8,128)}, f32[320,1280]{1,0:T(8,128)}, f32[320,512]{1,0:T(8,128)}) custom-call(f32[48,320]{1,0:T(8,128)} %get-tuple-element.12.refs_0_, f32[48,320]{1,0:T(8,128)} %get-tuple-element.13.refs_1_, f32[320,1280]{1,0:T(8,128)} %get-tuple-element.14.refs_2_, f32[320,512]{1,0:T(8,128)} %get-tuple-element.15.refs_3_), custom_call_target="tpu_custom_call" | custom-call | tf_op jit(solution)/shard_map/pallas_call | solution.py:666

commit v3 on v2

--- a/solution.py
+++ b/solution.py
@@ -15,8 +15,8 @@
 VC = 256
 MESH = pl.DeviceIdType.MESH
 HI = lax.Precision.HIGHEST
-PAIRS = 128
-SEMS = 256
+POOL = 64
+SEMS = 239
 f32 = jnp.float32
 bf16 = jnp.bfloat16
 
@@ -31,9 +31,9 @@
     trunk_in, embed_in, w, u, gain, ids_in, scale_in,
     tg_out, eg_out, cg_out, ug_out,
     tg, eg, cg, ug,
-    W2, XB, XS, PB, R2, T, Y8, MX, UP, LP, RL, MSC, YN, YS,
-    SB0, SY0, SB1, SY1, SB2, SZ2, GA, GS, GN, NB, NR, SG, DCB, DCR, SB3, SY3, RL2, TW,
-    GMF, GML, GMS, JP, RJ, SD, PRE, XPR, SB4, SY4, SB5, S7, VB, VR, VSB, VSR,
+    W2, XB, XS, PF, PB, R2, T, Y8, MX, UP, LP, RL, MSC, YN, YS,
+    SB0, SY0, SB1, SY1, SB2, SZ2, GA, GS, GN, NB, NR, INN, SB3, SY3, SB6, SZ6, RL2, TW,
+    GMF, GMB, GML, GMS, JP, RJ, RJ2, SD, PRE, XPR, SB4, SY4, SB5, SZ5, SB7, S7, VB, VR, VSB, VSR,
     ssem, rsem, lsem,
 ):
     h = lax.axis_index("head")
@@ -58,15 +58,15 @@
     right, left = dev(y_=add(y, 1, 8)), dev(y_=add(y, -1, 8))
     me = dev()
 
-    counts = {"both": 0, "s": PAIRS, "r": PAIRS}
-
-    def slots(n, which="both"):
-        first = counts[which]
-        counts[which] += n
+    counts = {"r": 0}
+
+    def slots(n):
+        first = counts["r"]
+        counts["r"] += n
         return first
 
     def some(sends, receives):
-        return slots(sends, "s"), slots(receives, "r")
+        return 0, slots(receives)
 
     finals = []
 
@@ -83,8 +83,11 @@
             pl.when(cond)(body)
 
     def send(src, dst, s, r, to, cond=None):
-        when(cond, lambda: copy(src(), dst(), s, r, to).start())
-        finals.append((cond, lambda: copy(src(), dst(), s, r, to).wait_send()))
+        at = len(finals) % POOL
+        if len(finals) >= POOL:
+            when(*finals[-POOL])
+        when(cond, lambda: copy(src(), dst(), at, r, to).start())
+        finals.append((cond, lambda: copy(src(), dst(), at, r, to).wait_send()))
 
     def recv(dst, r):
         copy(dst, dst, 0, r, me).wait_recv()
@@ -101,6 +104,18 @@
     def pick(x, at):
         ids = lax.broadcasted_iota(jnp.int32, x.shape, x.ndim - 1)
         return jnp.sum(jnp.where(ids == at, x, 0.0), axis=-1, keepdims=True)
+
+    def picks(x, at, n):
+        ids = lax.broadcasted_iota(jnp.int32, x.shape, x.ndim - 1)
+        return jnp.sum(jnp.where((ids >= at) & (ids < at + n), x, 0.0), axis=-1, keepdims=True)
+
+    def in_three(total, at, ids, rest):
+        high = total.astype(bf16).astype(f32)
+        middle = (total - high).astype(bf16).astype(f32)
+        low = total - high - middle
+        return jnp.where(
+            ids == at, high, jnp.where(ids == at + 1, middle, jnp.where(ids == at + 2, low, rest))
+        )
 
     def to_rows(first, second=None):
         ids = lax.broadcasted_iota(jnp.int32, (first.shape[0], 128), 1)
@@ -119,17 +134,17 @@
     barrier = pltpu.get_barrier_semaphore()
     peers = [dev(y_=add(y, j, 8)) for j in range(1, 8)]
     peers += [dev(z_=add(z, j, 8)) for j in range(1, 8)]
+    peers += [dev(y_=add(y, 4, 8), z_=add(z, j, 8)) for j in range(1, 8)]
     peers += [dev(h_=add(h, j, 4)) for j in range(1, 4)]
-    peers += [dev(h_=add(h, j, 4), z_=ozh * 4 + zl) for j in range(1, 4)]
     peers += [sib, dev(z_=ozh * 4 + zl, c_=oc)]
     for to in peers:
         pl.semaphore_signal(barrier, inc=1, device_id=to, device_id_type=MESH)
     own_w = pltpu.make_async_copy(w, W2.at[c], lsem.at[0])
     own_w.start()
     T[...] = jnp.zeros_like(T)
-    for ref in (SB0, SB1, SB2, SB3, SB4, SB5, DCB):
+    for ref in (SB0, SB1, SB2, SB3, SB4):
         ref[...] = jnp.zeros_like(ref)
-    PB[...] = jnp.zeros_like(PB)
+    PF[...] = jnp.zeros_like(PF)
     two = lax.broadcasted_iota(jnp.int32, (8, 384), 0)
     TW[...] = to_cols(
         jnp.where(two == 0, ids_in[...].astype(f32), jnp.where(two == 1, scale_in[...], 0.0))
@@ -141,19 +156,22 @@
     yq, ym = lax.div(y, 4), lax.rem(y, 4)
     hf = lax.rem(zl, 2)
     in_half = hf == yq
-    a_s, a_r = some(4, 8)
+    y_to = add(y, 4 * zh, 8)
+    first = jnp.where(in_half, 0, 4)
+    y_from = hf * 4 + ym
+    a_r = slots(4)
     for kind in range(2):
         for zh_to in range(2):
             z_to = zh_to * 4 + kind * 2 + yq
             send(
                 lambda kind=kind: (trunk_in, embed_in)[kind], lambda: XB.at[ym, z],
-                a_s + kind * 2 + zh_to, a_r + z, dev(z_=z_to), z_to != z,
+                0, a_r + zl, dev(y_=y_to, z_=z_to), (z_to != z) | (zh != 0),
             )
 
             def keep(kind=kind):
                 XB[ym, z] = (trunk_in, embed_in)[kind][...]
 
-            pl.when(z_to == z)(keep)
+            pl.when((z_to == z) & (zh == 0))(keep)
     w_s = slots(1)
     send(lambda: w, lambda: W2.at[c], w_s, w_s, sib)
 
@@ -170,22 +188,21 @@
 
     mine = quarter_of(h)
     b_s = slots(32)
-    for i in range(8):
+    for i in range(5):
         for unit in range(4):
             for way in range(2):
                 s = add(y, -i, 8) if way == 0 else add(y, i, 8)
                 k = lax.rem(s, 4)
-                cond = lax.div(s, 4) == hf
-                zs = way * 4 + unit
-                idx = b_s + k * 8 + zs
-                if i == 0:
-                    pl.when(in_half & (z != zs))(lambda: recv(XB.at[ym, zs], a_r + zs))
-                else:
-                    pl.when(cond)(lambda: recv(XB.at[k, zs], idx))
-                if i < 7:
+                zs = jnp.where(lax.div(s, 4) == hf, 0, 4) + unit
+                idx = b_s + (way * 4 + i) * 4 + unit
+                if i == 0 and way == 0:
+                    pl.when((zs != z) | (zh != 0))(lambda: recv(XB.at[ym, zs], a_r + unit))
+                if i > 0 and (i < 4 or unit // 2 == way):
+                    recv(XB.at[k, zs], idx - 4)
+                if i < 3 or (i == 3 and unit // 2 == way):
                     send(
                         lambda k=k, zs=zs: XB.at[k, zs], lambda k=k, zs=zs: XB.at[k, zs],
-                        idx, idx, right if way == 0 else left, cond,
+                        idx, idx, right if way == 0 else left,
                     )
         if i == 1:
             send(
@@ -211,9 +228,9 @@
         acc = acc + dot(block, W2[q // 4, :, (q % 4) * C : (q % 4 + 1) * C], 1, 1)
         wide = block.astype(f32)
         squares = squares + jnp.sum(wide * wide, axis=1, keepdims=True)
-    PB[:, :, 0:C] = acc.reshape(4, R, C)
+    PF[:, :, 0:C] = acc.reshape(4, R, C)
     lane3 = lax.broadcasted_iota(jnp.int32, (4, R, CP), 2)
-    PB[...] = jnp.where(lane3 >= C, squares.reshape(4, R, 1), PB[...])
+    PB[...] = in_three(squares.reshape(4, R, 1), C, lane3, PF[...]).astype(bf16)
     p_s, p_r = some(4, 4)
     for j in range(1, 4):
         zt = add(zl, j, 4)
@@ -226,20 +243,17 @@
     for j in range(1, 4):
         zt = add(zl, j, 4)
         recv(R2.at[zt], p_r + zt)
-    from_trunk = R2[0] + R2[1]
-    from_embed = R2[2] + R2[3]
+    from_trunk = R2[0].astype(f32) + R2[1].astype(f32)
+    from_embed = R2[2].astype(f32) + R2[3].astype(f32)
     trunk = trunk_in[...].astype(f32)
     embed = embed_in[...].astype(f32)
-    trunk_scale = lax.rsqrt(pick(from_trunk, C) / D + EPS)
-    embed_scale = lax.rsqrt(pick(from_embed, C) / D + EPS)
+    trunk_scale = lax.rsqrt(picks(from_trunk, C, 3) / D + EPS)
+    embed_scale = lax.rsqrt(picks(from_embed, C, 3) / D + EPS)
     mixed = trunk + trunk_scale * from_trunk[:, 0:C] + embed_scale * from_embed[:, 0:C]
-    MX[zl] = mixed
+    MX[...] = mixed
     gains = gain[...].reshape(1, C)
     total = jnp.sum(mixed * mixed, axis=1, keepdims=True)
-    high = total.astype(bf16).astype(f32)
-    middle = (total - high).astype(bf16).astype(f32)
-    low = total - high - middle
-    pieces = jnp.where(lane == C, high, jnp.where(lane == C + 1, middle, low))
+    pieces = in_three(total, C, lane, jnp.zeros((R, CP), f32))
     Y8[z] = widen(mixed * gains, pieces).astype(bf16)
     y_s, y_r = some(8, 8)
     for j in range(1, 8):
@@ -255,17 +269,9 @@
     for j in range(1, 8):
         zs = add(z, j, 8)
         recv(Y8.at[zs], y_r + zs)
-    m_s, m_r = some(4, 4)
-    for j in range(1, 4):
-        send(
-            lambda: MX.at[zl], lambda: MX.at[zl], m_s + j, m_r + zl, dev(z_=zh * 4 + add(zl, j, 4))
-        )
 
     wide = Y8[...].astype(f32)
-    ids = lax.broadcasted_iota(jnp.int32, wide.shape, 2)
-    split = jnp.sum(
-        jnp.where((ids >= C) & (ids < C + 3), wide, 0.0), axis=2, keepdims=True
-    )
+    split = picks(wide, C, 3)
     part_squares = (split[0:4] + split[4:8]).reshape(N, 1)
     SB0[:, 0:N] = to_rows(part_squares)
     s0_s, s0_r = some(8, 8)
@@ -372,16 +378,16 @@
     hits = (vocab_ids.astype(f32) == targets).astype(f32)
     GA[y] = (weights * (probs - hits)).astype(bf16)
 
-    g_s = slots(20)
+    g_s = slots(32)
     for i in range(5):
-        for way in range(2):
-            s = add(y, -i, 8) if way == 0 else add(y, i, 8)
-            for half in range(2):
-                rows = slice(half * 96, half * 96 + 96)
-                idx = g_s + (way * 5 + i) * 2 + half
-                if i > 0 and (i < 4 or half == way):
-                    recv(GA.at[s, rows], idx - 2)
-                if i < 3 or (i == 3 and half == way):
+        for unit in range(4):
+            for way in range(2):
+                s = add(y, -i, 8) if way == 0 else add(y, i, 8)
+                rows = slice(unit * R, unit * R + R)
+                idx = g_s + (way * 4 + i) * 4 + unit
+                if i > 0 and (i < 4 or unit // 2 == way):
+                    recv(GA.at[s, rows], idx - 4)
+                if i < 3 or (i == 3 and unit // 2 == way):
                     send(
                         lambda s=s, rows=rows: GA.at[s, rows], lambda s=s, rows=rows: GA.at[s, rows],
                         idx, idx, right if way == 0 else left,
@@ -406,27 +412,43 @@
         send(lambda zt=zt: NB.at[zt], lambda: NR.at[z], n8_s + j, n8_r + z, dev(z_=zt))
     NR[z] = NB[z]
 
+    held0 = Y8[0:4].reshape(N, CP)[:, 0:C].astype(f32)
+    held1 = Y8[4:8].reshape(N, CP)[:, 0:C].astype(f32)
+    SB3[:, 0:N] = to_rows(
+        jnp.sum(GN[0] * held0, axis=1, keepdims=True) + jnp.sum(GN[1] * held1, axis=1, keepdims=True)
+    )
+    s3_s, s3_r = some(8, 8)
+    for j in range(1, 8):
+        send(lambda: SB3, lambda: SY3.at[y], s3_s + j, s3_r + y, dev(y_=add(y, j, 8)))
+    SY3[y] = SB3[...]
+    for j in range(1, 8):
+        ys = add(y, j, 8)
+        recv(SY3.at[ys], s3_r + ys)
+    SB6[...] = jnp.sum(SY3[...], axis=0)
+    s6_s, s6_r = some(8, 8)
+    for j in range(1, 8):
+        send(lambda: SB6, lambda: SZ6.at[z], s6_s + j, s6_r + z, dev(z_=add(z, j, 8)))
+    SZ6[z] = SB6[...]
     for j in range(1, 8):
         zs = add(z, j, 8)
         recv(NR.at[zs], n8_r + zs)
-    for j in range(1, 4):
-        zs = add(zl, j, 4)
-        recv(MX.at[zs], m_r + zs)
-    grad_normed = jnp.sum(NR[...].astype(f32), axis=0)
-    scaled = grad_normed * gains
-    inner = jnp.sum(scaled * (MX[zl] * MSC[zl][:, 0:1]), axis=1, keepdims=True)
-    SG[zl] = widen(
-        scaled, jnp.where(lane == C, inner, jnp.where(lane == C + 1, trunk_scale, embed_scale))
-    )
-    DCB[:, 0:R] = to_rows(inner)
+    scaled = jnp.sum(NR[...].astype(f32), axis=0) * gains
+    scale_own = MSC[zl][:, 0:1]
+    mixed_normed = MX[...] * scale_own
+    for j in range(1, 8):
+        zs = add(z, j, 8)
+        recv(SZ6.at[zs], s6_r + zs)
+    INN[...] = to_cols(jnp.sum(SZ6[...], axis=0)[:, 0:N]).reshape(4, R, 128)
+    inner = scale_own * pick(INN[zl], 0)
+    grad_mixed = scale_own * (scaled - mixed_normed * (inner / D))
+    GMF[...] = grad_mixed
+    pieces = in_three(trunk_scale, C, lane, in_three(embed_scale, C + 3, lane, jnp.zeros((R, CP), f32)))
+    GMB[zl] = widen(grad_mixed, pieces).astype(bf16)
     d_s, d_r = some(4, 4)
-    e_s, e_r = some(4, 4)
     for j in range(1, 4):
         zt = add(zl, j, 4)
-        send(lambda: SG.at[zl], lambda: SG.at[zl], d_s + j, d_r + zl, dev(z_=zh * 4 + zt))
-    for j in range(4):
-        zt = add(zl, j, 4)
-        send(lambda: DCB, lambda: DCR.at[zl], e_s + j, e_r + zl, dev(z_=ozh * 4 + zt))
+        send(lambda: GMB.at[zl], lambda: GMB.at[zl], d_s + j, d_r + zl, dev(z_=zh * 4 + zt))
+
     recv(GS, gs_s)
     recv(YS, n_s)
     normed_mine = YN[c]
@@ -446,31 +468,11 @@
 
     for j in range(1, 4):
         zs = add(zl, j, 4)
-        recv(SG.at[zs], d_r + zs)
-    for j in range(4):
-        zs = add(zl, j, 4)
-        recv(DCR.at[zs], e_r + zs)
-    other = jnp.concatenate([to_cols(DCR[j][:, 0:R]) for j in range(4)], axis=0)
-    inner_part = pick(SG[...], C).reshape(N, 1) + pick(other, 0)
-    SB3[:, 0:N] = to_rows(inner_part)
-    s3_s, s3_r = some(8, 8)
-    for j in range(1, 8):
-        send(lambda: SB3, lambda: SY3.at[y], s3_s + j, s3_r + y, dev(y_=add(y, j, 8)))
-    SY3[y] = SB3[...]
-    for j in range(1, 8):
-        ys = add(y, j, 8)
-        recv(SY3.at[ys], s3_r + ys)
-    inner_all = pick(to_cols(jnp.sum(SY3[...], axis=0)[:, 0:N]), 0)
-    mixed_normed = MX[...].reshape(N, C) * MSC[...].reshape(N, 128)[:, 0:1]
-    scales = MSC[...].reshape(N, 128)[:, 0:1]
-    grad_mixed = scales * (
-        SG[...].reshape(N, CP)[:, 0:C] - mixed_normed * (inner_all / D)
-    )
-    GMF[...] = grad_mixed.reshape(4, R, C)
-    grad_low = grad_mixed.astype(bf16)
-    gathered = SG[...].reshape(N, CP)
-    joined_scale = jnp.where(lax.div(zl, 2) == 0, pick(gathered, C + 1), pick(gathered, C + 2))
-    grad_joined = (grad_mixed * joined_scale).astype(bf16)
+        recv(GMB.at[zs], d_r + zs)
+    gathered = GMB[...].reshape(N, CP)
+    grad_low = gathered[:, 0:C]
+    joined_scale = picks(gathered.astype(f32), C + 3 * lax.div(zl, 2), 3)
+    grad_joined = (grad_low.astype(f32) * joined_scale).astype(bf16)
     GML[...] = grad_joined
     c_s = slots(1)
     send(lambda: GML, lambda: GMS, c_s, c_s, sib)
@@ -490,38 +492,56 @@
         send(lambda: VSB, lambda: VSR, q_s, q_s, dev(z_=ozh * 4 + zl, c_=oc), donor)
 
     j_s = slots(32)
-    for i in range(8):
-        for unit in range(4):
-            for way in range(2):
-                to = add(y, -1 - i, 8) if way == 0 else add(y, 1 + i, 8)
-                k = lax.rem(to, 4)
-                cond = lax.div(to, 4) == hf
-                part = way * 4 + unit
-                idx = j_s + k * 8 + part
-
-                def take():
-                    recv(RJ.at[k, part], idx)
-                    JP[k, part] = (JP[k, part].astype(f32) + RJ[k, part].astype(f32)).astype(bf16)
-
-                if i > 0:
-                    pl.when(cond)(take)
-                if i < 7:
-                    send(
-                        lambda k=k, part=part: JP.at[k, part], lambda k=k, part=part: RJ.at[k, part],
-                        idx, idx, right if way == 0 else left, cond,
-                    )
-        if i == 0:
+
+    def grad_hop(o, way, unit, got):
+        to = add(y, o, 8) if way == 0 else add(y, -o, 8)
+        k = lax.rem(to, 4)
+        part = jnp.where(lax.div(to, 4) == hf, 0, 4) + unit
+        idx = j_s + (way * 4 + o) * 4 + unit
+        if got:
+            last = RJ2.at[unit] if (o == 0 and way == 1) else RJ.at[k, part]
+            recv(last, idx)
+            JP[k, part] = (JP[k, part].astype(f32) + last[...].astype(f32)).astype(bf16)
+        if o:
+            place = RJ2.at[unit] if (o == 1 and way == 1) else RJ.at[k, part]
+            send(
+                lambda: JP.at[k, part], lambda: place, idx - 4, idx - 4,
+                right if way == 0 else left,
+            )
+
+    for unit in range(2):
+        grad_hop(4, 0, unit, False)
+        grad_hop(4, 1, unit + 2, False)
+    for unit in range(2):
+        grad_hop(3, 0, unit + 2, False)
+        grad_hop(3, 1, unit, False)
+    for unit in range(2):
+        grad_hop(3, 0, unit, True)
+        grad_hop(3, 1, unit + 2, True)
+    for o in (2, 1, 0):
+        for unit in (2, 3, 0, 1):
+            grad_hop(o, 0, unit, True)
+            grad_hop(o, 1, (unit + 2) % 4, True)
+        if o == 1:
             sum_vocab()
     kind_mine = lax.div(zl, 2)
-    k_s, k_r = some(8, 4)
-    for j in range(1, 8):
-        zt = add(z, j, 8)
+    k_r = slots(4)
+    for part in range(4):
+        z_to = first + part
         send(
-            lambda zt=zt: JP.at[ym, zt], lambda: SD.at[kind_mine, zh], k_s + j,
-            k_r + kind_mine * 2 + zh, dev(z_=zt), in_half,
+            lambda z_to=z_to: JP.at[ym, z_to], lambda: SD.at[kind_mine, zh], 0,
+            k_r + kind_mine * 2 + zh, dev(y_=y_from, z_=z_to), jnp.logical_not(in_half & (z_to == z)),
         )
 
-    @pl.when(in_half)
+    held = pl.ds(first, 4)
+    raw = jnp.sum(JP[ym, held].astype(f32) * XB[ym, held].astype(f32), axis=2, keepdims=True)
+    SB4[:, 0:N] = to_rows(raw.reshape(N, 1))
+    s4_s, s4_r = some(8, 8)
+    for j in range(1, 8):
+        send(lambda: SB4, lambda: SY4.at[y], s4_s + j, s4_r + y, dev(y_=add(y, j, 8)))
+    SY4[y] = SB4[...]
+
+    @pl.when(in_half & (zh == 0))
     def _():
         SD[kind_mine, zh] = JP[ym, z]
 
@@ -537,57 +557,57 @@
             ) + dot(grad_sib, XS[kk, part].reshape(N, C), 0, 0)
 
     put(2).start()
+    for j in range(1, 8):
+        ys = add(y, j, 8)
+        recv(SY4.at[ys], s4_r + ys)
+    SB5[...] = jnp.sum(SY4[...], axis=0)
+    s5_s, s5_r = some(8, 8)
+    for j in range(1, 8):
+        send(lambda: SB5, lambda: SZ5.at[z], s5_s + j, s5_r + z, dev(z_=add(z, j, 8)))
+    SZ5[z] = SB5[...]
     for kind in range(2):
         for zs in range(2):
             z_from = zs * 4 + kind * 2 + yq
-            pl.when(z_from != z)(lambda: recv(SD.at[kind, zs], k_r + kind * 2 + zs))
+            pl.when((z_from != z) | (zh != 0))(lambda: recv(SD.at[kind, zs], k_r + kind * 2 + zs))
     trunk_side = SD[0, 0].astype(f32) + SD[0, 1].astype(f32)
     embed_side = SD[1, 0].astype(f32) + SD[1, 1].astype(f32)
     trunk_normed = trunk * trunk_scale
     embed_normed = embed * embed_scale
-    PRE[...] = GMF[zl] + trunk_scale * trunk_side
-    SB4[:, 0:R] = to_rows(
-        jnp.sum(trunk_side * trunk_normed, axis=1, keepdims=True),
-        jnp.sum(embed_side * embed_normed, axis=1, keepdims=True),
-    )
-    s4_s, s4_r = some(8, 8)
-    for j in range(1, 8):
-        send(lambda: SB4, lambda: SY4.at[y], s4_s + j, s4_r + y, dev(y_=add(y, j, 8)))
-    SY4[y] = SB4[...]
+    before = GMF[...] + trunk_scale * trunk_side
+    PRE[...] = before.astype(bf16)
     o_s, o_r = some(4, 4)
     for j in range(1, 4):
         send(lambda: PRE, lambda: XPR.at[h], o_s + j, o_r + h, dev(h_=add(h, j, 4)))
     XPR[h] = PRE[...]
-
-    for j in range(1, 8):
-        ys = add(y, j, 8)
-        recv(SY4.at[ys], s4_r + ys)
-    SB5[...] = jnp.sum(SY4[...], axis=0)
-    s5_s, s5_r = some(8, 8)
-    for j in range(4):
-        for flip in range(2):
-            if j + flip:
-                send(
-                    lambda: SB5, lambda: S7.at[h, zh], s5_s + j * 2 + flip, s5_r + h * 2 + zh,
-                    dev(h_=add(h, j, 4), z_=(ozh if flip else zh) * 4 + zl),
-                )
-    S7[h, zh] = SB5[...]
-    for j in range(4):
-        for flip in range(2):
-            if j + flip:
-                hs, zs = add(h, j, 4), (ozh if flip else zh)
-                recv(S7.at[hs, zs], s5_r + hs * 2 + zs)
-    every = jnp.sum(S7[...], axis=(0, 1))
-    same = S7[h, 0] + S7[h, 1]
-    ids = lax.broadcasted_iota(jnp.int32, (8, 128), 0)
-    dots = to_cols(jnp.where(ids == 0, every, same)[:, 0:R])
+    for j in range(1, 8):
+        zs = add(z, j, 8)
+        recv(SZ5.at[zs], s5_r + zs)
+    ids = lax.broadcasted_iota(jnp.int32, (8, VC), 0)
+    SB7[...] = jnp.where(
+        ids == 0,
+        (SZ5[0] + SZ5[1] + SZ5[4] + SZ5[5])[0:1],
+        jnp.where(ids == 1, (SZ5[2] + SZ5[3] + SZ5[6] + SZ5[7])[0:1], 0.0),
+    )
+    s7_s, s7_r = some(4, 4)
+    for j in range(1, 4):
+        send(lambda: SB7, lambda: S7.at[h], s7_s + j, s7_r + h, dev(h_=add(h, j, 4)))
+    S7[h] = SB7[...]
     pl.when(owner)(lambda: put(3).start())
-    eg[...] = embed_scale * (embed_side - embed_normed * (pick(dots, 1) / D))
+    for j in range(1, 4):
+        hs = add(h, j, 4)
+        recv(S7.at[hs], s7_r + hs)
+    INN[...] = to_cols(
+        jnp.where(ids == 0, jnp.sum(S7[...], axis=0), S7[h])[:, 0:N]
+    ).reshape(4, R, 128)
+    dots = INN[zl]
+    eg[...] = embed_scale * (embed_side - embed_normed * (embed_scale * pick(dots, 1) / D))
     put(1).start()
     for j in range(1, 4):
         hs = add(h, j, 4)
         recv(XPR.at[hs], o_r + hs)
-    tg[...] = jnp.sum(XPR[...], axis=0) - trunk_scale * trunk_normed * (pick(dots, 0) / D)
+    tg[...] = jnp.sum(XPR[...].astype(f32), axis=0) - trunk_scale * trunk_normed * (
+        trunk_scale * pick(dots, 0) / D
+    )
 
     put(0).start()
 
@@ -599,8 +619,8 @@
 
     for at in range(4):
         put(at).wait()
-    assert counts["both"] <= PAIRS and max(counts.values()) <= SEMS
-    for cond, body in finals:
+    assert counts["r"] <= SEMS
+    for cond, body in finals[-POOL:]:
         when(cond, body)
 
 
@@ -625,17 +645,19 @@
     vb = lambda *shape: pltpu.VMEM(shape, bf16)
     scratch = [
         vm(R, C), vm(R, C), vm(C, 1280), vm(C, 512),
-        vb(2, C, 1280), vb(4, 8, R, C), vb(2, 8, R, C), vm(4, R, CP), vm(4, R, CP), vm(R, CP),
-        vb(8, R, CP), vm(4, R, C), vb(2, C, V), vm(8, N, VC), vm(8, N, VC), vm(4, R, 128),
+        vb(2, C, 1280), vb(4, 8, R, C), vb(2, 8, R, C), vm(4, R, CP), vb(4, R, CP), vb(4, R, CP), vm(R, CP),
+        vb(8, R, CP), vm(R, C), vb(2, C, V), vm(8, N, VC), vm(8, N, VC), vm(4, R, 128),
         vb(2, N, C), vb(N, C),
         vm(8, VC), vm(8, 8, VC), vm(8, VC), vm(8, 8, VC), vm(8, VC), vm(8, 8, VC),
         vb(8, N, VC), vb(8, N, VC), vm(2, N, C), vb(8, R, C), vb(8, R, C),
-        vm(4, R, CP), vm(8, 128), vm(4, 8, 128), vm(8, VC), vm(8, 8, VC),
+        vm(4, R, 128), vm(8, VC), vm(8, 8, VC), vm(8, VC), vm(8, 8, VC),
         vm(N, VC), vm(4, 2, R, 128),
-        vm(4, R, C), vb(N, C), vb(N, C), vb(4, 8, R, C), vb(4, 8, R, C), vb(2, 2, R, C),
-        vm(R, C), vm(4, R, C), vm(8, 128), vm(8, 8, 128), vm(8, 128), vm(4, 2, 8, 128),
+        vm(R, C), vb(4, R, CP), vb(N, C), vb(N, C),
+        vb(4, 8, R, C), vb(4, 8, R, C), vb(4, R, C), vb(2, 2, R, C),
+        vb(R, C), vb(4, R, C), vm(8, VC), vm(8, 8, VC), vm(8, VC), vm(8, 8, VC),
+        vm(8, VC), vm(4, 8, VC),
         vb(4, C, 512), vb(4, C, 512), vb(C, 512), vb(C, 512),
-        pltpu.SemaphoreType.DMA((SEMS,)), pltpu.SemaphoreType.DMA((SEMS,)), pltpu.SemaphoreType.DMA((6,)),
+        pltpu.SemaphoreType.DMA((POOL,)), pltpu.SemaphoreType.DMA((SEMS,)), pltpu.SemaphoreType.DMA((6,)),
     ]
     spec = pl.BlockSpec(memory_space=pltpu.VMEM)
     remote = pl.BlockSpec(memory_space=pl.ANY)

time: 182 us -> 157 us (0.86)
  Pallas kernels: 181 us -> 157 us
    pallas_call x1, Pallas kernels: 178 us -> 154 us  [local(): pl.pallas_call(kernel, out_shape=(jax.ShapeDtypeStruct((R, C), f32), jax....]
where the time goes in v3:
time: 157 us
  Pallas kernels  157 us (100%)
    pallas_call x1, Pallas kernels, local(): pl.pallas_call(kernel, out_shape=(jax.ShapeDtypeStruct((R, C), f32), jax....  154 us

profile of v3, /device:TPU:56, one launch (start us, length us, event | category | flops | bytes accessed | tf_op | source)
XLA Modules:
  0.0 157.2 jit_solution(4692032267090972578)
XLA Ops:
  0.6 153.6 %shard_map.102 = (f32[48,320]{1,0:T(8,128)}, f32[48,320]{1,0:T(8,128)}, f32[320,1280]{1,0:T(8,128)}, f32[320,512]{1,0:T(8,128)}) custom-call(bf16[48,320]{1,0:T(8,128)(2,1)} %trunk_in.1, bf16[48,320]{1,0:T(8,128)(2,1)} %bitcast.14, bf16[320,1280]{1,0:T(8,128)(2,1)} %bitcast.13, bf16[320,2048]{1,0:T(8,128)(2,1)} %bitcast.12, f32[320]{0:T(512)} %gain.1, ...), custom_call_target="tpu_custom_call" | custom-call | tf_op jit(solution)/shard_map/pallas_call | solution.py:664
  154.3 2.9 %shard_map.103 = (f32[48,320]{1,0:T(8,128)}, f32[48,320]{1,0:T(8,128)}, f32[320,1280]{1,0:T(8,128)}, f32[320,512]{1,0:T(8,128)}) custom-call(f32[48,320]{1,0:T(8,128)} %get-tuple-element.12.refs_0_, f32[48,320]{1,0:T(8,128)} %get-tuple-element.13.refs_1_, f32[320,1280]{1,0:T(8,128)} %get-tuple-element.14.refs_2_, f32[320,512]{1,0:T(8,128)} %get-tuple-element.15.refs_3_), custom_call_target="tpu_custom_call" | custom-call | tf_op jit(solution)/shard_map/pallas_call | solution.py:688

commit v4 on v3

--- a/solution.py
+++ b/solution.py
@@ -16,7 +16,7 @@
 MESH = pl.DeviceIdType.MESH
 HI = lax.Precision.HIGHEST
 POOL = 64
-SEMS = 239
+SEMS = 246
 f32 = jnp.float32
 bf16 = jnp.bfloat16
 
@@ -180,6 +180,7 @@
     u_f = slots(1)
     u_x, u_q = some(9, 4)
     u_b, u_d = u_x + 4, u_x + 8
+    send(lambda: u, lambda: UP.at[zh], u_f, u_f, sib, owner)
     own_u = lambda: pltpu.make_async_copy(u, UP.at[zh], lsem.at[1])
     pl.when(owner)(lambda: own_u().start())
 
@@ -204,20 +205,19 @@
                         lambda k=k, zs=zs: XB.at[k, zs], lambda k=k, zs=zs: XB.at[k, zs],
                         idx, idx, right if way == 0 else left,
                     )
-        if i == 1:
+        if i == 0:
             send(
                 lambda: u.at[:, mine], lambda: UP.at[zh, :, mine], u_d, u_q + h,
                 dev(z_=ozh * 4 + zl), donor,
             )
-
-    send(lambda: u, lambda: UP.at[zh], u_f, u_f, sib, owner)
-    pl.when(owner)(lambda: recv(UP.at[ozh, :, mine], u_q + h))
-    for j in range(1, 4):
-        send(
-            lambda: UP.at[ozh, :, mine], lambda: UP.at[ozh, :, mine], u_x + j, u_q + h,
-            dev(h_=add(h, j, 4)), owner,
-        )
-    send(lambda: UP.at[ozh, :, mine], lambda: UP.at[ozh, :, mine], u_b, u_q + h, sib, owner)
+        if i == 3:
+            pl.when(owner)(lambda: recv(UP.at[ozh, :, mine], u_q + h))
+            for j in range(1, 4):
+                send(
+                    lambda: UP.at[ozh, :, mine], lambda: UP.at[ozh, :, mine], u_x + j, u_q + h,
+                    dev(h_=add(h, j, 4)), owner,
+                )
+            send(lambda: UP.at[ozh, :, mine], lambda: UP.at[ozh, :, mine], u_b, u_q + h, sib, owner)
 
     own_w.wait()
     recv(W2.at[oc], w_s)
@@ -238,8 +238,6 @@
             lambda zt=zt: PB.at[zt], lambda: R2.at[zl], p_s + j, p_r + zl, dev(z_=zh * 4 + zt)
         )
     R2[zl] = PB[zl]
-    x_s = slots(1)
-    send(lambda: XB.at[pl.ds(2 * oc, 2)], lambda: XS, x_s, x_s, sib)
     for j in range(1, 4):
         zt = add(zl, j, 4)
         recv(R2.at[zt], p_r + zt)
@@ -269,6 +267,9 @@
     for j in range(1, 8):
         zs = add(z, j, 8)
         recv(Y8.at[zs], y_r + zs)
+
+    x_s = slots(1)
+    send(lambda: XB.at[pl.ds(2 * oc, 2)], lambda: XS, x_s, x_s, sib)
 
     wide = Y8[...].astype(f32)
     split = picks(wide, C, 3)
@@ -378,6 +379,18 @@
     hits = (vocab_ids.astype(f32) == targets).astype(f32)
     GA[y] = (weights * (probs - hits)).astype(bf16)
 
+    def normed_block(at, fresh=False):
+        rows = pl.ds(pl.multiple_of(at * VC, VC), VC)
+        grads = GA[at]
+        for zc in range(2):
+            value = dot(grads, UP[zc, :, rows], 1, 1)
+            GN[zc] = value if fresh else GN[zc] + value
+
+    gs_s = slots(8)
+
+    def to_sibling(at):
+        send(lambda: GA.at[at], lambda: GS.at[at], 0, gs_s + at, sib)
+
     g_s = slots(32)
     for i in range(5):
         for unit in range(4):
@@ -392,19 +405,12 @@
                         lambda s=s, rows=rows: GA.at[s, rows], lambda s=s, rows=rows: GA.at[s, rows],
                         idx, idx, right if way == 0 else left,
                     )
-    gs_s = slots(1)
-    send(lambda: GA, lambda: GS, gs_s, gs_s, sib)
-
-    GN[...] = jnp.zeros_like(GN)
-
-    def normed_block(at, carry):
-        rows = pl.ds(pl.multiple_of(at * VC, VC), VC)
-        grads = GA[at]
-        for zc in range(2):
-            GN[zc] += dot(grads, UP[zc, :, rows], 1, 1)
-        return carry
-
-    lax.fori_loop(0, 8, normed_block, 0)
+        arrived = {0: (y,), 4: (add(y, 4, 8),)}.get(i, (add(y, -i, 8), add(y, i, 8)))
+        for at in arrived:
+            to_sibling(at)
+        for at in arrived:
+            normed_block(at, i == 0)
+
     NB[...] = GN[...].astype(bf16).reshape(8, R, C)
     n8_s, n8_r = some(8, 8)
     for j in range(1, 8):
@@ -429,6 +435,25 @@
     for j in range(1, 8):
         send(lambda: SB6, lambda: SZ6.at[z], s6_s + j, s6_r + z, dev(z_=add(z, j, 8)))
     SZ6[z] = SB6[...]
+
+    for j in range(8):
+        recv(GS.at[j], gs_s + j)
+    recv(YS, n_s)
+    normed_mine = YN[c]
+    normed_sib = YS[...]
+
+    def vocab_block(at, carry):
+        value = dot(normed_mine, GA[at], 0, 0) + dot(normed_sib, GS[at], 0, 0)
+        VB[lax.div(at, 2), :, pl.ds(pl.multiple_of(lax.rem(at, 2) * VC, VC), VC)] = value.astype(bf16)
+        return carry
+
+    lax.fori_loop(0, 8, vocab_block, 0)
+    v_s, v_r = some(4, 4)
+    for j in range(1, 4):
+        ht = add(h, j, 4)
+        send(lambda ht=ht: VB.at[ht], lambda: VR.at[h], v_s + j, v_r + h, dev(h_=ht))
+    VR[h] = VB[h]
+
     for j in range(1, 8):
         zs = add(z, j, 8)
         recv(NR.at[zs], n8_r + zs)
@@ -448,23 +473,6 @@
     for j in range(1, 4):
         zt = add(zl, j, 4)
         send(lambda: GMB.at[zl], lambda: GMB.at[zl], d_s + j, d_r + zl, dev(z_=zh * 4 + zt))
-
-    recv(GS, gs_s)
-    recv(YS, n_s)
-    normed_mine = YN[c]
-    normed_sib = YS[...]
-
-    def vocab_block(at, carry):
-        value = dot(normed_mine, GA[at], 0, 0) + dot(normed_sib, GS[at], 0, 0)
-        VB[lax.div(at, 2), :, pl.ds(pl.multiple_of(lax.rem(at, 2) * VC, VC), VC)] = value.astype(bf16)
-        return carry
-
-    lax.fori_loop(0, 8, vocab_block, 0)
-    v_s, v_r = some(4, 4)
-    for j in range(1, 4):
-        ht = add(h, j, 4)
-        send(lambda ht=ht: VB.at[ht], lambda: VR.at[h], v_s + j, v_r + h, dev(h_=ht))
-    VR[h] = VB[h]
 
     for j in range(1, 4):
         zs = add(zl, j, 4)
@@ -522,7 +530,7 @@
         for unit in (2, 3, 0, 1):
             grad_hop(o, 0, unit, True)
             grad_hop(o, 1, (unit + 2) % 4, True)
-        if o == 1:
+        if o == 2:
             sum_vocab()
     kind_mine = lax.div(zl, 2)
     k_r = slots(4)

time: 157 us -> 156 us (level)
  Pallas kernels: 157 us -> 154 us
    pallas_call x1, Pallas kernels: 154 us -> 151 us  [local(): pl.pallas_call(kernel, out_shape=(jax.ShapeDtypeStruct((R, C), f32), jax....]
where the time goes in v4:
time: 156 us; the launch traced here: 155 us
  Pallas kernels  154 us (99%)
    pallas_call x1, Pallas kernels, local(): pl.pallas_call(kernel, out_shape=(jax.ShapeDtypeStruct((R, C), f32), jax....  151 us

profile of v4, /device:TPU:56, one launch (start us, length us, event | category | flops | bytes accessed | tf_op | source)
XLA Modules:
  0.0 154.9 jit_solution(2815849331003354789)
XLA Ops:
  0.6 151.3 %shard_map.102 = (f32[48,320]{1,0:T(8,128)}, f32[48,320]{1,0:T(8,128)}, f32[320,1280]{1,0:T(8,128)}, f32[320,512]{1,0:T(8,128)}) custom-call(bf16[48,320]{1,0:T(8,128)(2,1)} %trunk_in.1, bf16[48,320]{1,0:T(8,128)(2,1)} %bitcast.14, bf16[320,1280]{1,0:T(8,128)(2,1)} %bitcast.13, bf16[320,2048]{1,0:T(8,128)(2,1)} %bitcast.12, f32[320]{0:T(512)} %gain.1, ...), custom_call_target="tpu_custom_call" | custom-call | tf_op jit(solution)/shard_map/pallas_call | solution.py:672
  152.0 2.9 %shard_map.103 = (f32[48,320]{1,0:T(8,128)}, f32[48,320]{1,0:T(8,128)}, f32[320,1280]{1,0:T(8,128)}, f32[320,512]{1,0:T(8,128)}) custom-call(f32[48,320]{1,0:T(8,128)} %get-tuple-element.12.refs_0_, f32[48,320]{1,0:T(8,128)} %get-tuple-element.13.refs_1_, f32[320,1280]{1,0:T(8,128)} %get-tuple-element.14.refs_2_, f32[320,512]{1,0:T(8,128)} %get-tuple-element.15.refs_3_), custom_call_target="tpu_custom_call" | custom-call | tf_op jit(solution)/shard_map/pallas_call | solution.py:696

commit v5 on v4

--- a/solution.py
+++ b/solution.py
@@ -15,8 +15,8 @@
 VC = 256
 MESH = pl.DeviceIdType.MESH
 HI = lax.Precision.HIGHEST
-POOL = 64
-SEMS = 246
+POOL = 48
+SEMS = 266
 f32 = jnp.float32
 bf16 = jnp.bfloat16
 
@@ -33,7 +33,7 @@
     tg, eg, cg, ug,
     W2, XB, XS, PF, PB, R2, T, Y8, MX, UP, LP, RL, MSC, YN, YS,
     SB0, SY0, SB1, SY1, SB2, SZ2, GA, GS, GN, NB, NR, INN, SB3, SY3, SB6, SZ6, RL2, TW,
-    GMF, GMB, GML, GMS, JP, RJ, RJ2, SD, PRE, XPR, SB4, SY4, SB5, SZ5, SB7, S7, VB, VR, VSB, VSR,
+    GMF, GMB, GML, GMS, JP, RJ, RJ2, SD, PRE, XPR, SB4, SY4, SB5, S5, VB, VR, VSB, VSR,
     ssem, rsem, lsem,
 ):
     h = lax.axis_index("head")
@@ -135,7 +135,7 @@
     peers = [dev(y_=add(y, j, 8)) for j in range(1, 8)]
     peers += [dev(z_=add(z, j, 8)) for j in range(1, 8)]
     peers += [dev(y_=add(y, 4, 8), z_=add(z, j, 8)) for j in range(1, 8)]
-    peers += [dev(h_=add(h, j, 4)) for j in range(1, 4)]
+    peers += [dev(h_=add(h, i, 4), z_=add(z, j, 8)) for i in range(1, 4) for j in range(8)]
     peers += [sib, dev(z_=ozh * 4 + zl, c_=oc)]
     for to in peers:
         pl.semaphore_signal(barrier, inc=1, device_id=to, device_id_type=MESH)
@@ -569,10 +569,15 @@
         ys = add(y, j, 8)
         recv(SY4.at[ys], s4_r + ys)
     SB5[...] = jnp.sum(SY4[...], axis=0)
-    s5_s, s5_r = some(8, 8)
-    for j in range(1, 8):
-        send(lambda: SB5, lambda: SZ5.at[z], s5_s + j, s5_r + z, dev(z_=add(z, j, 8)))
-    SZ5[z] = SB5[...]
+    s5_r = slots(32)
+    for i in range(4):
+        for j in range(8):
+            if i + j:
+                send(
+                    lambda: SB5, lambda: S5.at[h, z], 0, s5_r + h * 8 + z,
+                    dev(h_=add(h, i, 4), z_=add(z, j, 8)), zl < 2 if i else None,
+                )
+    S5[h, z] = SB5[...]
     for kind in range(2):
         for zs in range(2):
             z_from = zs * 4 + kind * 2 + yq
@@ -587,25 +592,20 @@
     for j in range(1, 4):
         send(lambda: PRE, lambda: XPR.at[h], o_s + j, o_r + h, dev(h_=add(h, j, 4)))
     XPR[h] = PRE[...]
-    for j in range(1, 8):
-        zs = add(z, j, 8)
-        recv(SZ5.at[zs], s5_r + zs)
+    pl.when(owner)(lambda: put(3).start())
+    for i in range(4):
+        for j in range(8):
+            if i + j:
+                hs, zs = add(h, i, 4), add(z, j, 8)
+                when(
+                    lax.rem(zs, 4) < 2 if i else None,
+                    lambda: recv(S5.at[hs, zs], s5_r + hs * 8 + zs),
+                )
     ids = lax.broadcasted_iota(jnp.int32, (8, VC), 0)
-    SB7[...] = jnp.where(
-        ids == 0,
-        (SZ5[0] + SZ5[1] + SZ5[4] + SZ5[5])[0:1],
-        jnp.where(ids == 1, (SZ5[2] + SZ5[3] + SZ5[6] + SZ5[7])[0:1], 0.0),
-    )
-    s7_s, s7_r = some(4, 4)
-    for j in range(1, 4):
-        send(lambda: SB7, lambda: S7.at[h], s7_s + j, s7_r + h, dev(h_=add(h, j, 4)))
-    S7[h] = SB7[...]
-    pl.when(owner)(lambda: put(3).start())
-    for j in range(1, 4):
-        hs = add(h, j, 4)
-        recv(S7.at[hs], s7_r + hs)
+    of_trunk = jnp.sum(S5[:, 0] + S5[:, 1] + S5[:, 4] + S5[:, 5], axis=0)[0:1]
+    of_embed = (S5[h, 2] + S5[h, 3] + S5[h, 6] + S5[h, 7])[0:1]
     INN[...] = to_cols(
-        jnp.where(ids == 0, jnp.sum(S7[...], axis=0), S7[h])[:, 0:N]
+        jnp.where(ids == 0, of_trunk, jnp.where(ids == 1, of_embed, 0.0))[:, 0:N]
     ).reshape(4, R, 128)
     dots = INN[zl]
     eg[...] = embed_scale * (embed_side - embed_normed * (embed_scale * pick(dots, 1) / D))
@@ -634,16 +634,23 @@
 
 def put_out(*refs):
     into, out, held, sems = refs[:4], refs[4:8], refs[8:12], refs[12]
-    reads = [pltpu.make_async_copy(into[k], held[k], sems.at[k]) for k in range(4)]
-    writes = [pltpu.make_async_copy(held[k], out[k], sems.at[k + 4]) for k in range(4)]
-    order = (2, 3, 0, 1)
-    for k in order:
-        reads[k].start()
-    for k in order:
-        reads[k].wait()
-        writes[k].start()
-    for k in order:
-        writes[k].wait()
+    parts = [(2, slice(80 * n, 80 * n + 80)) for n in range(4)]
+    parts += [(3, slice(0, 160)), (3, slice(160, 320)), (0, slice(0, R)), (1, slice(0, R))]
+
+    def move(n, ins):
+        k, rows = parts[n]
+        source, target = (into, held) if ins else (held, out)
+        return pltpu.make_async_copy(
+            source[k].at[rows], target[k].at[rows], sems.at[n + (0 if ins else 8)]
+        )
+
+    for n in range(8):
+        move(n, True).start()
+    for n in range(8):
+        move(n, True).wait()
+        move(n, False).start()
+    for n in range(8):
+        move(n, False).wait()
 
 
 def local(
@@ -662,8 +669,7 @@
         vm(N, VC), vm(4, 2, R, 128),
         vm(R, C), vb(4, R, CP), vb(N, C), vb(N, C),
         vb(4, 8, R, C), vb(4, 8, R, C), vb(4, R, C), vb(2, 2, R, C),
-        vb(R, C), vb(4, R, C), vm(8, VC), vm(8, 8, VC), vm(8, VC), vm(8, 8, VC),
-        vm(8, VC), vm(4, 8, VC),
+        vb(R, C), vb(4, R, C), vm(8, VC), vm(8, 8, VC), vm(8, VC), vm(4, 8, 8, VC),
         vb(4, C, 512), vb(4, C, 512), vb(C, 512), vb(C, 512),
         pltpu.SemaphoreType.DMA((POOL,)), pltpu.SemaphoreType.DMA((SEMS,)), pltpu.SemaphoreType.DMA((6,)),
     ]
@@ -699,7 +705,7 @@
         in_specs=[remote] * 4,
         out_specs=(remote,) * 4,
         scratch_shapes=[pltpu.VMEM(r.shape, r.dtype) for r in results]
-        + [pltpu.SemaphoreType.DMA((8,))],
+        + [pltpu.SemaphoreType.DMA((16,))],
         compiler_params=pltpu.CompilerParams(vmem_limit_bytes=60 * 1024 * 1024),
     )(*results)
     return trunk_grad, embed_grad[None], combine_grad.T[None], unembed_grad.T[None, None]

time: 156 us -> 155 us (level)
  Pallas kernels: 154 us -> 152 us
    pallas_call x1, Pallas kernels: 151 us -> 149 us  [local(): pl.pallas_call(kernel, out_shape=(jax.ShapeDtypeStruct((R, C), f32), jax....]
where the time goes in v5:
time: 155 us; the launch traced here: 153 us
  Pallas kernels  152 us (98%)
    pallas_call x1, Pallas kernels, local(): pl.pallas_call(kernel, out_shape=(jax.ShapeDtypeStruct((R, C), f32), jax....  149 us

profile of v5, /device:TPU:56, one launch (start us, length us, event | category | flops | bytes accessed | tf_op | source)
XLA Modules:
  0.0 152.7 jit_solution(6755304507348664992)
XLA Ops:
  0.6 149.5 %shard_map.102 = (f32[48,320]{1,0:T(8,128)}, f32[48,320]{1,0:T(8,128)}, f32[320,1280]{1,0:T(8,128)}, f32[320,512]{1,0:T(8,128)}) custom-call(bf16[48,320]{1,0:T(8,128)(2,1)} %trunk_in.1, bf16[48,320]{1,0:T(8,128)(2,1)} %bitcast.14, bf16[320,1280]{1,0:T(8,128)(2,1)} %bitcast.13, bf16[320,2048]{1,0:T(8,128)(2,1)} %bitcast.12, f32[320]{0:T(512)} %gain.1, ...), custom_call_target="tpu_custom_call" | custom-call | tf_op jit(solution)/shard_map/pallas_call | solution.py:678
  150.1 2.6 %shard_map.103 = (f32[48,320]{1,0:T(8,128)}, f32[48,320]{1,0:T(8,128)}, f32[320,1280]{1,0:T(8,128)}, f32[320,512]{1,0:T(8,128)}) custom-call(f32[48,320]{1,0:T(8,128)} %get-tuple-element.12.refs_0_, f32[48,320]{1,0:T(8,128)} %get-tuple-element.13.refs_1_, f32[320,1280]{1,0:T(8,128)} %get-tuple-element.14.refs_2_, f32[320,512]{1,0:T(8,128)} %get-tuple-element.15.refs_3_), custom_call_target="tpu_custom_call" | custom-call | tf_op jit(solution)/shard_map/pallas_call | solution.py:702
